TPU v7x, 256 devices: a whole 4x4x8 slice. The times are simulated.
256 devices in a mesh: pair: 8 (over y_lo, x), feat: 32 (over y_hi, z, core).
Axes of the slice: x: 4, y: 4 (y_hi: 2, y_lo: 2; y = y_hi * 2 + y_lo), z: 8, core: 2. Of those that a mesh axis runs over, the one named last changes fastest.
Arguments:
- decoder: float32 [8, 16384, 2048], P('pair', 'feat'), may hold values from -0.3125 to 0.3125
- pair_map: int32 [8, 2], P('pair'), may hold values from 0 to 3, as said below
- indices: int32 [3, 256, 128], replicated, may hold values from 0 to 16383, as said below
- values: float32 [3, 256, 128], replicated, may hold values from 0.2 to 3
- target: float32 [3, 256, 2048], P(None, ('pair', 'feat')), may hold values from -6 to 6
Outputs:
- recon: bfloat16 [3, 256, 2048], P(None, ('pair', 'feat'))
- dec_grad: float32 [8, 16384, 2048], P('pair', 'feat')
- feat_grad: float32 [3, 256, 128], P(None, ('pair', 'feat'))
Inputs may be any that keep to these rules, and one draw needn't show every extreme that they name: `pair_map`: each pair (s, t) of layers with s <= t < 3 stands in exactly one row as (s, t); every other row is (3, 3), an empty slot. For each layer and token the 128 indices are distinct.
All inputs are finite; a program needn't handle non-finite values.
Results may differ from a plain program's by a relative error of at most 0.0027.
Values may be sent and summed in bfloat16 or wider, within the bound.
A program may use at most 128 MiB of HBM per device.

v0:
```python
import jax
import jax.numpy as jnp
from jax import lax
from jax.sharding import PartitionSpec as P


def pick_layer(stack, chosen_layer):
    layer_ids = jnp.arange(stack.shape[0], dtype=jnp.int32)[:, None, None]
    return jnp.sum(jnp.where(layer_ids == chosen_layer, stack, jnp.zeros_like(stack)), axis=0)


def body(decoder, pair_map, indices, values, target):
    slot_count, block_width, model_width = decoder.shape
    layers = indices.shape[0]
    first_feature = lax.axis_index("feat") * block_width
    columns = jnp.arange(block_width, dtype=jnp.int32)
    sources = pair_map[:, 0]
    goals = pair_map[:, 1]
    slot_index = 0
    picked = jnp.minimum(sources[slot_index], layers - 1)
    local_ids = pick_layer(indices, picked) - first_feature
    weights = pick_layer(values, picked)
    matches = (local_ids[:, :, None] == columns).astype(jnp.float32)
    active = jnp.einsum(
        "tk,tkf->tf",
        weights,
        matches,
        precision=lax.Precision.HIGHEST,
        preferred_element_type=jnp.float32,
    )
    product = jnp.dot(
        active,
        decoder[slot_index],
        precision=lax.Precision.HIGHEST,
        preferred_element_type=jnp.float32,
    )
    local_list = [local_ids]
    active_list = [active]
    product_list = [product]
    stacked = jnp.stack(product_list)
    choose_goal = jax.nn.one_hot(goals, layers, dtype=jnp.float32)
    choose_narrow = choose_goal.astype(jnp.bfloat16)
    layer_term = jnp.einsum(
        "jl,jtd->ltd",
        choose_goal,
        stacked,
        precision=lax.Precision.HIGHEST,
        preferred_element_type=jnp.float32,
    )
    shares = lax.psum_scatter(layer_term, ("pair", "feat"), scatter_dimension=1, tiled=True)
    error_share = (shares - target).astype(jnp.bfloat16)
    error_full = lax.all_gather(error_share, ("pair", "feat"), axis=1, tiled=True)
    slot_errors = jnp.einsum(
        "jl,ltd->jtd", choose_narrow, error_full, preferred_element_type=jnp.float32
    ).astype(jnp.bfloat16)
    recon = shares.astype(jnp.bfloat16)
    slot_index = 0
    slot_error = slot_errors[slot_index].astype(jnp.float32)
    tile_grad = jnp.dot(
        active_list[slot_index].T,
        slot_error,
        precision=lax.Precision.HIGHEST,
        preferred_element_type=jnp.float32,
    )
    grad_list = [tile_grad]
    back = jnp.dot(
        slot_error,
        decoder[slot_index].T,
        precision=lax.Precision.HIGHEST,
        preferred_element_type=jnp.float32,
    )
    matches = (local_list[slot_index][:, :, None] == columns).astype(jnp.float32)
    picked_grad = jnp.einsum(
        "tkf,tf->tk",
        matches,
        back,
        precision=lax.Precision.HIGHEST,
        preferred_element_type=jnp.float32,
    )
    choose_source = jax.nn.one_hot(sources[slot_index], layers, dtype=jnp.float32)
    feature_term = choose_source[:, None, None] * picked_grad[None]
    dec_grad = jnp.stack(grad_list)
    feat_grad = lax.psum_scatter(feature_term, ("pair", "feat"), scatter_dimension=1, tiled=True)
    return (recon, dec_grad, feat_grad)


def solution(mesh):
    in_specs = (P("pair", "feat", None), P("pair", None), P(), P(), P(None, ("pair", "feat"), None))
    out_specs = (
        P(None, ("pair", "feat"), None),
        P("pair", "feat", None),
        P(None, ("pair", "feat"), None),
    )
    return jax.shard_map(body, mesh=mesh, in_specs=in_specs, out_specs=out_specs, check_vma=False)
```

profile of v0, /device:TPU:1, one launch (start us, length us, event | category | flops | bytes accessed | tf_op | source)
XLA Modules:
  0.0 1047.7 jit_solution(10654120748516346442)
XLA Ops:
  7.2 0.0 all-reduce.5.cloned.1.call-start
  7.2 1.3 fusion.18
  9.2 1.1 select_reduce_fusion
  10.3 1.1 select_reduce_fusion.1
  11.4 0.7 compare_convert_fusion.1
  12.1 0.0 copy-start
  12.1 23.2 %fusion.1 = f32[256,1,512]{2,1,0:T(1,128)S(1)} fusion(f32[256,128,1]{1,2,0:T(1,128)S(1)} %bitcast.32, s32[256,128]{1,0:T(8,128)S(1)} %broadcast_subtract_fusion), kind=kOutput, calls=%fused_computation.2 | convolution fusion | flops 218103808 | bytes 786432 | tf_op jit(solution)/shard_map/tk,tkf->tf/dot_general | solution.py:24
  35.3 0.0 copy-done
  35.3 3.7 fusion.6
  39.0 5.7 broadcast_multiply_fusion
  44.7 0.0 copy-start.2
  44.7 0.0 all-reduce.5.cloned.1.call-update
  44.7 0.0 all-gather.2.cloned.1.call-start
  44.8 282.1 %all-reduce.5.cloned.1.call-done = f32[3,256,2048]{2,0,1:T(4,128)} async-done(((f32[3,256,2048]{2,0,1:T(4,128)}), f32[3,256,2048]{2,0,1:T(4,128)}) %all-reduce.5.cloned.1.call-update) | async-done | bytes 6291472
  326.9 0.0 copy-done.2
  326.9 1.4 fusion.16
  328.2 0.0 all-gather.2.cloned.1.call-update
  328.3 0.2 all-reduce.7.cloned.1.call-start
  328.5 0.7 compare_convert_fusion
  329.1 1.4 dynamic-slice_convert_fusion
  330.5 415.4 %all-gather.2.cloned.1.call-done = bf16[3,256,2048]{2,0,1:T(4,128)(2,1)} async-done(((bf16[3,1,2048]{2,0,1:T(4,128)(2,1)}), bf16[3,256,2048]{2,0,1:T(4,128)(2,1)}) %all-gather.2.cloned.1.call-update) | async-done | bytes 3145744 | tf_op jit(solution)/shard_map/all_gather | solution.py:52
  745.9 0.0 copy-start.1
  745.9 5.5 fusion.17
  751.3 0.0 copy-done.1
  751.4 2.6 fusion.8
  754.0 32.3 %fusion = f32[256,1,128]{2,1,0:T(1,128)S(1)} fusion(s32[256,128]{1,0:T(8,128)S(1)} %broadcast_subtract_fusion, f32[256,512,1]{1,0,2:T(8,128)S(1)} %fusion.8), kind=kOutput, calls=%fused_computation.1 | convolution fusion | flops 218103808 | bytes 786432 | tf_op jit(solution)/shard_map/tkf,tf->tk/dot_general | solution.py:73
  786.3 1.0 broadcast_multiply_fusion.1
  787.3 0.0 all-reduce.7.cloned.1.call-update
  787.3 4.1 convolution_bitcast_fusion
  791.4 248.5 %all-reduce.7.cloned.1.call-done = f32[3,256,128]{2,0,1:T(4,128)} async-done(((f32[3,256,128]{2,0,1:T(4,128)}), f32[3,256,128]{2,0,1:T(4,128)}) %all-reduce.7.cloned.1.call-update) | async-done | bytes 393232
  1039.9 0.7 constant_dynamic-slice_fusion
  1040.6 0.6 copy.10
  (2 shorter events, 0.0 us)
Async XLA Ops:
  7.2 319.7 %all-reduce.5.cloned.1.call-start = ((), (), s32[]{:S(2)}) async-start(), calls=%async_computation.1 | async-start | bytes 16777216
  12.1 23.2 %copy-start = (f32[1,512,2048]{2,1,0:T(8,128)S(1)}, f32[1,512,2048]{2,1,0:T(8,128)}, u32[]{:S(2)}) copy-start(f32[1,512,2048]{2,1,0:T(8,128)} %param.5) | copy-start | bytes 12582916
  44.7 282.2 %copy-start.2 = (f32[3,1,2048]{2,1,0:T(1,128)S(1)}, f32[3,1,2048]{2,1,0:T(1,128)}, u32[]{:S(2)}) copy-start(f32[3,1,2048]{2,1,0:T(1,128)} %param.9) | copy-start | bytes 73732
  44.7 701.2 %all-gather.2.cloned.1.call-start = ((), (), s32[]{:S(2)}) async-start(), calls=%async_computation | async-start | bytes 4210688 | tf_op jit(solution)/shard_map/all_gather | solution.py:52
  328.3 711.6 %all-reduce.7.cloned.1.call-start = ((), (), s32[]{:S(2)}) async-start(), calls=%async_computation.2 | async-start | bytes 1048576
  745.9 5.5 copy-start.1
Sparse Core Ops, SparseCore 0:
  44.8 281.9 all-reduce.4
  329.3 416.5 all-gather.1
  787.4 252.4 all-reduce.6
where the time goes:
time: 1050 us
  waiting for transfers between devices  946 us (90%)
  matrix products  71.4 us (7%)
  between operations  14.5 us (1%)
  other arithmetic  11.5 us (1%)
    unnamed x5, waiting for transfers between devices  531 us
    all_gather x1, waiting for transfers between devices, body(): lax.all_gather(error_share, ('pair', 'feat'), axis=1, tiled=True)  415 us
    dot_general x1, matrix products, body(): jnp.einsum('tkf,tf->tk', matches, back, precision=lax.Precision.HIGHEST,...  32.3 us
    dot_general x1, matrix products, body(): jnp.einsum('tk,tkf->tf', weights, matches, precision=lax.Precision.HIGHES...  23.2 us
  transfers between devices with their start and end apart: 3, of which 3 were waited for; matrix products, arithmetic and copies ran while one was open for 1% of the time, Pallas kernels for 0%

commit v1 on v0

v1 whole, which is shorter than its diff:
```python
import jax
import jax.numpy as jnp
from jax import lax
from jax.experimental import pallas as pl
from jax.experimental.pallas import tpu as pltpu
from jax.sharding import PartitionSpec as P

MESH = pl.DeviceIdType.MESH
F32 = jnp.float32
BF16 = jnp.bfloat16

LAYERS = 3
TOK = 256
ACTIVE = 128
WIDTH = 512
MODEL = 2048
HALF = MODEL // 2
PAIRS = 8
PLANE = 16
LINE = 16
ROWS = TOK // PLANE


def split(x):
    high = x.astype(BF16)
    return high, (x - high.astype(F32)).astype(BF16)


def nt(a, b):
    return lax.dot_general(a, b, (((1,), (1,)), ((), ())), preferred_element_type=F32)


def exchange_kernel(
    pair_map, indices, values, target, decoder,
    recon, feat, error_out, acts_high_t, acts_low_t,
    dec, dec_high, dec_low, ids_t, vals_t, acts_t, acts_high, acts_low,
    map_send, map_rx, part_send, part_rx, part_own, plane_rx, layer_sum,
    line_send, line_rx, err_send, err_rx, err_wide, err_layers, err_pick, err,
    back, picked, pick_rx, pick_line, feat_rx,
    dec_sem, map_ssem, map_rsem, part_ssem, part_rsem, plane_ssem, plane_rsem,
    line_ssem, line_rsem, err_ssem, err_rsem, spread_ssem, spread_rsem,
    relay_ssem, relay_rsem, pick_ssem, pick_rsem, feat_ssem, feat_rsem,
):
    p = lax.axis_index("pair")
    f = lax.axis_index("feat")
    y = f // 16
    w = lax.rem(f, 16)
    core = lax.rem(f, 2)
    q = p * 2 + y

    def plane_peer(d):
        q2 = lax.rem(q + d, PLANE)
        return q2, (q2 // 2, lax.rem(q2, 2) * 16 + w)

    def line_peer(d):
        w2 = lax.rem(w + d, LINE)
        return w2, (p, y * 16 + w2)

    partner = (p, f + 1 - 2 * core)

    for block in range(4):
        cols = pl.ds(block * 512, 512)
        pltpu.make_async_copy(
            decoder.at[0, :, cols], dec.at[:, cols], dec_sem.at[block]
        ).start()

    barrier = pltpu.get_barrier_semaphore()

    @pl.loop(1, 16)
    def _(d):
        pl.semaphore_signal(barrier, inc=1, device_id=plane_peer(d)[1], device_id_type=MESH)
        pl.semaphore_signal(barrier, inc=1, device_id=line_peer(d)[1], device_id_type=MESH)

    pl.semaphore_wait(barrier, 30)

    source = pair_map[0, 0]
    goal = pair_map[0, 1]
    row = lax.broadcasted_iota(jnp.int32, (8, 128), 0)
    tile = jnp.where(row < 4, source, goal)
    map_send[...] = tile
    map_rx[p] = tile

    def map_copy(d):
        p2 = lax.rem(p + d, PAIRS)
        return pltpu.make_async_remote_copy(
            src_ref=map_send, dst_ref=map_rx.at[p], send_sem=map_ssem.at[p2],
            recv_sem=map_rsem.at[p], device_id=(p2, f), device_id_type=MESH)

    def map_arrival(d):
        p2 = lax.rem(p + d, PAIRS)
        return pltpu.make_async_remote_copy(
            src_ref=map_send, dst_ref=map_rx.at[p2], send_sem=map_ssem.at[p],
            recv_sem=map_rsem.at[p2], device_id=(p2, f), device_id_type=MESH)

    @pl.loop(1, PAIRS)
    def _(d):
        map_copy(d).start()

    layer = jnp.minimum(source, LAYERS - 1)
    local = indices[layer] - f * WIDTH
    ids_t[...] = local.T
    vals_t[...] = values[layer].T

    @pl.loop(0, WIDTH // 64)
    def _(block):
        base = block * 64
        features = lax.broadcasted_iota(jnp.int32, (64, TOK), 0) + base

        def step(k, total):
            for j in range(4):
                ids = ids_t[pl.ds(k * 4 + j, 1), :]
                vals = vals_t[pl.ds(k * 4 + j, 1), :]
                total = jnp.where(ids == features, vals, total)
            return total

        total = lax.fori_loop(0, ACTIVE // 4, step, jnp.zeros((64, TOK), F32))
        acts_t[pl.ds(base, 64), :] = total
        high, low = split(total)
        acts_high_t[pl.ds(base, 64), :] = high
        acts_low_t[pl.ds(base, 64), :] = low

    for block in range(WIDTH // 128):
        cols = slice(block * 128, block * 128 + 128)
        high, low = split(acts_t[cols, :].T)
        acts_high[:, cols] = high
        acts_low[:, cols] = low

    for block in range(4):
        cols = pl.ds(block * 512, 512)
        pltpu.make_async_copy(
            decoder.at[0, :, cols], dec.at[:, cols], dec_sem.at[block]
        ).wait()

    @pl.loop(0, WIDTH // 16)
    def _(block):
        rows = pl.ds(block * 16, 16)
        high, low = split(dec[rows, :])
        dec_high[rows, :] = high
        dec_low[rows, :] = low

    def partial(cols):
        high = dec_high[:, cols]
        return (
            jnp.dot(acts_high[...], high, preferred_element_type=F32)
            + jnp.dot(acts_low[...], high, preferred_element_type=F32)
            + jnp.dot(acts_high[...], dec_low[:, cols], preferred_element_type=F32)
        )

    part_copy = pltpu.make_async_remote_copy(
        src_ref=part_send, dst_ref=part_rx, send_sem=part_ssem, recv_sem=part_rsem,
        device_id=partner, device_id_type=MESH)

    @pl.loop(0, HALF // 256)
    def _(n):
        cols = pl.ds(pl.multiple_of((1 - core) * HALF + n * 256, 256), 256)
        part_send[:, pl.ds(pl.multiple_of(n * 256, 256), 256)] = partial(cols)

    part_copy.start()

    @pl.loop(0, HALF // 256)
    def _(n):
        cols = pl.ds(pl.multiple_of(core * HALF + n * 256, 256), 256)
        part_own[:, pl.ds(pl.multiple_of(n * 256, 256), 256)] = partial(cols)

    part_copy.wait()

    def rows_of(q2):
        return pl.ds(pl.multiple_of(q2 * ROWS, ROWS), ROWS)

    def plane_copy(d):
        q2, peer = plane_peer(d)
        return pltpu.make_async_remote_copy(
            src_ref=part_own.at[rows_of(q2)], dst_ref=plane_rx.at[q], send_sem=plane_ssem.at[q2],
            recv_sem=plane_rsem.at[q], device_id=peer, device_id_type=MESH)

    def plane_arrival(q2):
        return pltpu.make_async_remote_copy(
            src_ref=part_own.at[rows_of(q2)], dst_ref=plane_rx.at[q2], send_sem=plane_ssem.at[q],
            recv_sem=plane_rsem.at[q2], device_id=partner, device_id_type=MESH)

    @pl.loop(1, PLANE)
    def _(d):
        rows = rows_of(lax.rem(q + d, PLANE))
        part_own[rows, :] = part_own[rows, :] + part_rx[rows, :]
        plane_copy(d).start()

    plane_rx[q] = part_own[rows_of(q), :] + part_rx[rows_of(q), :]

    @pl.loop(1, PAIRS)
    def _(d):
        map_arrival(d).wait_recv()

    @pl.loop(1, PLANE)
    def _(d):
        plane_arrival(lax.rem(q + d, PLANE)).wait_recv()

    layer_sum[...] = jnp.zeros_like(layer_sum)

    @pl.loop(0, PAIRS)
    def _(p2):
        both = plane_rx[2 * p2] + plane_rx[2 * p2 + 1]
        goal2 = map_rx[p2, 4:5, 0:1]
        for l in range(LAYERS):
            layer_sum[l] += jnp.where(goal2 == l, both, 0.0)

    for l in range(LAYERS):
        for m in range(8):
            line_send[pl.ds(l * 8 + m, 16, stride=24), :] = layer_sum[l, :, m * 128:m * 128 + 128]

    def tile_of(w2):
        return pl.ds(pl.multiple_of(w2 * 24, 8), 24)

    def line_copy(d):
        w2, peer = line_peer(d)
        return pltpu.make_async_remote_copy(
            src_ref=line_send.at[tile_of(w2)], dst_ref=line_rx.at[w], send_sem=line_ssem.at[w2],
            recv_sem=line_rsem.at[w], device_id=peer, device_id_type=MESH)

    def line_arrival(w2):
        return pltpu.make_async_remote_copy(
            src_ref=line_send.at[tile_of(w2)], dst_ref=line_rx.at[w2], send_sem=line_ssem.at[w],
            recv_sem=line_rsem.at[w2], device_id=partner, device_id_type=MESH)

    @pl.loop(1, LINE)
    def _(d):
        line_copy(d).start()

    line_rx[w] = line_send[tile_of(w), :]

    @pl.loop(1, LINE)
    def _(d):
        line_arrival(lax.rem(w + d, LINE)).wait_recv()

    for half in range(2):
        total = line_rx[half]
        for z2 in range(1, 8):
            total = total + line_rx[2 * z2 + half]
        for l in range(LAYERS):
            part = total[l * 8:l * 8 + 8]
            rows = slice(half * 8, half * 8 + 8)
            recon[l, rows, :] = part.astype(BF16)
            err_send[half, l * 8:l * 8 + 8, :] = (part - target[l, rows, :]).astype(BF16)
        err_send[half, 24:32, :] = jnp.zeros((8, 128), BF16)

    def err_copy(d):
        w2, peer = line_peer(d)
        return pltpu.make_async_remote_copy(
            src_ref=err_send.at[lax.rem(w2, 2)], dst_ref=err_rx.at[w], send_sem=err_ssem.at[w2],
            recv_sem=err_rsem.at[w], device_id=peer, device_id_type=MESH)

    def err_arrival(w2):
        return pltpu.make_async_remote_copy(
            src_ref=err_send.at[0], dst_ref=err_rx.at[w2], send_sem=err_ssem.at[w],
            recv_sem=err_rsem.at[w2], device_id=partner, device_id_type=MESH)

    @pl.loop(1, LINE)
    def _(d):
        err_copy(d).start()

    err_rx[w] = err_send[core]

    @pl.loop(1, LINE)
    def _(d):
        err_arrival(lax.rem(w + d, LINE)).wait_recv()

    @pl.loop(0, LINE)
    def _(w2):
        err_wide[pl.ds(pl.multiple_of(w2 * 32, 32), 32), :] = err_rx[w2].astype(F32)

    for l in range(LAYERS):
        for m in range(8):
            err_layers[l, :, m * 128:m * 128 + 128] = err_wide[pl.ds(l * 8 + m, 16, stride=32), :]

    @pl.loop(0, PAIRS)
    def _(p2):
        goal2 = map_rx[p2, 4:5, 0:1]
        chosen = jnp.zeros((ROWS, HALF), F32)
        for l in range(LAYERS):
            chosen = jnp.where(goal2 == l, err_layers[l], chosen)
        err_pick[p2] = chosen.astype(BF16)

    def spread_copy(d):
        q2, peer = plane_peer(d)
        return pltpu.make_async_remote_copy(
            src_ref=err_pick.at[q2 // 2], dst_ref=err.at[core, rows_of(q)], send_sem=spread_ssem.at[q2],
            recv_sem=spread_rsem.at[q], device_id=peer, device_id_type=MESH)

    def spread_arrival(q2):
        return pltpu.make_async_remote_copy(
            src_ref=err_pick.at[0], dst_ref=err.at[core, rows_of(q2)], send_sem=spread_ssem.at[q],
            recv_sem=spread_rsem.at[q2], device_id=partner, device_id_type=MESH)

    def relay_copy(q2):
        piece = err.at[core, rows_of(q2)]
        return pltpu.make_async_remote_copy(
            src_ref=piece, dst_ref=piece, send_sem=relay_ssem.at[q2],
            recv_sem=relay_rsem.at[q2], device_id=partner, device_id_type=MESH)

    def relay_arrival(q2):
        piece = err.at[1 - core, rows_of(q2)]
        return pltpu.make_async_remote_copy(
            src_ref=piece, dst_ref=piece, send_sem=relay_ssem.at[q2],
            recv_sem=relay_rsem.at[q2], device_id=partner, device_id_type=MESH)

    @pl.loop(1, PLANE)
    def _(d):
        spread_copy(d).start()

    err[core, rows_of(q), :] = err_pick[p]
    relay_copy(q).start()

    @pl.loop(1, PLANE)
    def _(d):
        q2 = lax.rem(q + d, PLANE)
        spread_arrival(q2).wait_recv()
        relay_copy(q2).start()

    @pl.loop(0, PLANE)
    def _(q2):
        relay_arrival(q2).wait_recv()

    error_out[...] = err[...]

    @pl.loop(0, WIDTH // 128)
    def _(n):
        rows = pl.ds(pl.multiple_of(n * 128, 128), 128)
        total = jnp.zeros((TOK, 128), F32)
        for half in range(2):
            cols = slice(half * HALF, half * HALF + HALF)
            total = total + nt(err[half], dec_high[rows, cols]) + nt(err[half], dec_low[rows, cols])
        back[n] = total

    local = indices[layer] - f * WIDTH
    lane = jnp.bitwise_and(local, 127)
    block_of = jnp.right_shift(local, 7)
    found = jnp.zeros((TOK, ACTIVE), F32)
    for n in range(WIDTH // 128):
        here = jnp.take_along_axis(back[n], lane, axis=1)
        found = jnp.where(block_of == n, here, found)
    picked[...] = found

    def pick_copy(d):
        q2, peer = plane_peer(d)
        return pltpu.make_async_remote_copy(
            src_ref=picked.at[rows_of(q2)], dst_ref=pick_rx.at[q], send_sem=pick_ssem.at[q2],
            recv_sem=pick_rsem.at[q], device_id=peer, device_id_type=MESH)

    def pick_arrival(q2):
        return pltpu.make_async_remote_copy(
            src_ref=picked.at[rows_of(q2)], dst_ref=pick_rx.at[q2], send_sem=pick_ssem.at[q],
            recv_sem=pick_rsem.at[q2], device_id=partner, device_id_type=MESH)

    @pl.loop(1, PLANE)
    def _(d):
        pick_copy(d).start()

    pick_rx[q] = picked[rows_of(q), :]
    pick_line[...] = jnp.zeros_like(pick_line)

    @pl.loop(1, PLANE)
    def _(d):
        pick_arrival(lax.rem(q + d, PLANE)).wait_recv()

    sums = [jnp.zeros((ROWS, ACTIVE), F32) for _ in range(LAYERS)]
    for p2 in range(PAIRS):
        both = pick_rx[2 * p2] + pick_rx[2 * p2 + 1]
        source2 = map_rx[p2, 0:1, 0:1]
        for l in range(LAYERS):
            sums[l] = sums[l] + jnp.where(source2 == l, both, 0.0)
    for l in range(LAYERS):
        pick_line[pl.ds(l, 16, stride=8), :] = sums[l]

    def feat_copy(d):
        w2, peer = line_peer(d)
        return pltpu.make_async_remote_copy(
            src_ref=pick_line.at[pl.ds(pl.multiple_of(w2 * 8, 8), 8)], dst_ref=feat_rx.at[w],
            send_sem=feat_ssem.at[w2], recv_sem=feat_rsem.at[w], device_id=peer, device_id_type=MESH)

    def feat_arrival(w2):
        return pltpu.make_async_remote_copy(
            src_ref=pick_line.at[pl.ds(0, 8)], dst_ref=feat_rx.at[w2],
            send_sem=feat_ssem.at[w], recv_sem=feat_rsem.at[w2], device_id=partner, device_id_type=MESH)

    @pl.loop(1, LINE)
    def _(d):
        feat_copy(d).start()

    feat_rx[w] = pick_line[pl.ds(pl.multiple_of(w * 8, 8), 8), :]

    @pl.loop(1, LINE)
    def _(d):
        feat_arrival(lax.rem(w + d, LINE)).wait_recv()

    total = feat_rx[0]
    for w2 in range(1, LINE):
        total = total + feat_rx[w2]
    feat[...] = total[0:LAYERS]

    @pl.loop(1, PAIRS)
    def _(d):
        map_copy(d).wait_send()

    @pl.loop(1, 16)
    def _(d):
        plane_copy(d).wait_send()
        line_copy(d).wait_send()
        err_copy(d).wait_send()
        spread_copy(d).wait_send()
        pick_copy(d).wait_send()
        feat_copy(d).wait_send()

    @pl.loop(0, PLANE)
    def _(q2):
        relay_copy(q2).wait_send()


def grad_kernel(acts_high_t, acts_low_t, err, out):
    e = err[0]
    out[...] = (
        jnp.dot(acts_high_t[...], e, preferred_element_type=F32)
        + jnp.dot(acts_low_t[...], e, preferred_element_type=F32)
    )


def body(decoder, pair_map, indices, values, target):
    vmem = pl.BlockSpec(memory_space=pltpu.VMEM)
    dma = pltpu.SemaphoreType.DMA
    recon, feat, err, acts_high_t, acts_low_t = pl.pallas_call(
        exchange_kernel,
        out_shape=(
            jax.ShapeDtypeStruct((LAYERS, 16, 128), BF16),
            jax.ShapeDtypeStruct((LAYERS, ACTIVE), F32),
            jax.ShapeDtypeStruct((2, TOK, HALF), BF16),
            jax.ShapeDtypeStruct((WIDTH, TOK), BF16),
            jax.ShapeDtypeStruct((WIDTH, TOK), BF16),
        ),
        in_specs=[pl.BlockSpec(memory_space=pltpu.SMEM), vmem, vmem, vmem, pl.BlockSpec(memory_space=pl.ANY)],
        out_specs=(vmem,) * 5,
        scratch_shapes=[
            pltpu.VMEM((WIDTH, MODEL), F32),
            pltpu.VMEM((WIDTH, MODEL), BF16),
            pltpu.VMEM((WIDTH, MODEL), BF16),
            pltpu.VMEM((ACTIVE, TOK), jnp.int32),
            pltpu.VMEM((ACTIVE, TOK), F32),
            pltpu.VMEM((WIDTH, TOK), F32),
            pltpu.VMEM((TOK, WIDTH), BF16),
            pltpu.VMEM((TOK, WIDTH), BF16),
            pltpu.VMEM((8, 128), jnp.int32),
            pltpu.VMEM((PAIRS, 8, 128), jnp.int32),
            pltpu.VMEM((TOK, HALF), F32),
            pltpu.VMEM((TOK, HALF), F32),
            pltpu.VMEM((TOK, HALF), F32),
            pltpu.VMEM((PLANE, ROWS, HALF), F32),
            pltpu.VMEM((LAYERS, ROWS, HALF), F32),
            pltpu.VMEM((LINE * 24, 128), F32),
            pltpu.VMEM((LINE, 24, 128), F32),
            pltpu.VMEM((2, 32, 128), BF16),
            pltpu.VMEM((LINE, 32, 128), BF16),
            pltpu.VMEM((LINE * 32, 128), F32),
            pltpu.VMEM((LAYERS, ROWS, HALF), F32),
            pltpu.VMEM((PAIRS, ROWS, HALF), BF16),
            pltpu.VMEM((2, TOK, HALF), BF16),
            pltpu.VMEM((WIDTH // 128, TOK, 128), F32),
            pltpu.VMEM((TOK, ACTIVE), F32),
            pltpu.VMEM((PLANE, ROWS, ACTIVE), F32),
            pltpu.VMEM((LINE * 8, 128), F32),
            pltpu.VMEM((LINE, 8, 128), F32),
            dma((4,)),
            dma((PAIRS,)), dma((PAIRS,)),
            dma, dma,
            dma((PLANE,)), dma((PLANE,)),
            dma((LINE,)), dma((LINE,)),
            dma((LINE,)), dma((LINE,)),
            dma((PLANE,)), dma((PLANE,)),
            dma((PLANE,)), dma((PLANE,)),
            dma((PLANE,)), dma((PLANE,)),
            dma((LINE,)), dma((LINE,)),
        ],
        compiler_params=pltpu.CompilerParams(
            collective_id=0, has_side_effects=True, vmem_limit_bytes=56 * 2**20
        ),
    )(pair_map, indices, values, target.reshape(LAYERS, 16, 128), decoder)
    dec_grad = pl.pallas_call(
        grad_kernel,
        grid=(8,),
        out_shape=jax.ShapeDtypeStruct((WIDTH, MODEL), F32),
        in_specs=[
            pl.BlockSpec((WIDTH, TOK), lambda n: (0, 0)),
            pl.BlockSpec((WIDTH, TOK), lambda n: (0, 0)),
            pl.BlockSpec((1, TOK, 256), lambda n: (n // 4, 0, n % 4)),
        ],
        out_specs=pl.BlockSpec((WIDTH, 256), lambda n: (0, n)),
    )(acts_high_t, acts_low_t, err)
    return (
        recon.reshape(LAYERS, 1, MODEL),
        dec_grad.reshape(1, WIDTH, MODEL),
        feat.reshape(LAYERS, 1, ACTIVE),
    )


def solution(mesh):
    in_specs = (P("pair", "feat", None), P("pair", None), P(), P(), P(None, ("pair", "feat"), None))
    out_specs = (
        P(None, ("pair", "feat"), None),
        P("pair", "feat", None),
        P(None, ("pair", "feat"), None),
    )
    return jax.shard_map(body, mesh=mesh, in_specs=in_specs, out_specs=out_specs, check_vma=False)
```

time: 1050 us -> 89.8 us (0.09)
  waiting for transfers between devices: 946 us -> 0 us
  Pallas kernels: 0 us -> 87.8 us
  matrix products: 71.4 us -> 0 us
  between operations: 14.5 us -> 0.66 us
  other arithmetic: 11.5 us -> 0 us
    unnamed x5 -> x0, waiting for transfers between devices: 531 us -> none
    all_gather x1 -> x0, waiting for transfers between devices: 415 us -> none  [body(): lax.all_gather(error_share, ('pair', 'feat'), axis=1, tiled=True)]
    pallas_call x0 -> x2, Pallas kernels: none -> 87.8 us  [the longest x1 80.7 us: body(): pl.pallas_call(exchange_kernel, out_shape=(jax.ShapeDtypeStruct((LAYERS,...]
    dot_general x6 -> x0, matrix products: 71.4 us -> none  [the longest x1 32.3 us: body(): jnp.einsum('tkf,tf->tk', matches, back, precision=lax.Precision.HIGHEST,...]
  transfers between devices with their start and end apart: 3 -> 0, of which waited for: 3 -> 0; matrix products, arithmetic and copies ran while one was open for 1% -> 0% of each run, Pallas kernels for 0% -> 0%
where the time goes in v1:
time: 89.8 us; the launch traced here: 89.6 us
  Pallas kernels  87.8 us (98%)
  local copies, waits for them, and re-layouts  1.19 us (1%)
    pallas_call x1, Pallas kernels, body(): pl.pallas_call(exchange_kernel, out_shape=(jax.ShapeDtypeStruct((LAYERS,...  80.7 us
    pallas_call x1, Pallas kernels, body(): pl.pallas_call(grad_kernel, grid=(8,), out_shape=jax.ShapeDtypeStruct((WI...  7.06 us

profile of v1, /device:TPU:1, one launch (start us, length us, event | category | flops | bytes accessed | tf_op | source)
XLA Modules:
  0.0 89.6 jit_solution(8839280136985806429)
XLA Ops:
  0.6 80.7 %shard_map.76 = (bf16[3,16,128]{2,1,0:T(8,128)(2,1)}, f32[3,128]{1,0:T(4,128)}, bf16[2,256,1024]{2,1,0:T(8,128)(2,1)}, bf16[512,256]{1,0:T(8,128)(2,1)}, bf16[512,256]{1,0:T(8,128)(2,1)}) custom-call(s32[1,2]{1,0:T(1,128)} %pair_map.1, s32[3,256,128]{2,1,0:T(8,128)} %indices.1, f32[3,256,128]{2,1,0:T(8,128)} %values.1, f32[3,16,128]{2,1,0:T(8,128)} %bitcast.4, ...), custom_call_target="tpu_custom_call" | custom-call | tf_op jit(solution)/shard_map/pallas_call | solution.py:428
  81.3 0.0 copy-start
  81.3 0.0 copy-start.1
  81.4 7.1 %shard_map.77 = f32[512,2048]{1,0:T(8,128)} custom-call(bf16[512,256]{1,0:T(8,128)(2,1)} %get-tuple-element.9.acts_high_t, bf16[512,256]{1,0:T(8,128)(2,1)} %get-tuple-element.10.acts_low_t, bf16[2,256,1024]{2,1,0:T(8,128)(2,1)} %get-tuple-element.11.err), custom_call_target="tpu_custom_call" | custom-call | tf_op jit(solution)/shard_map/pallas_call | solution.py:483
  88.4 0.0 copy-done
  88.4 0.6 reshape.19
  89.0 0.0 copy-done.1
  89.0 0.6 copy.8
Async XLA Ops:
  81.3 7.1 %copy-start = (bf16[3,16,128]{2,1,0:T(8,128)(2,1)S(1)}, bf16[3,16,128]{2,1,0:T(8,128)(2,1)}, u32[]{:S(2)}) copy-start(bf16[3,16,128]{2,1,0:T(8,128)(2,1)} %get-tuple-element.8) | copy-start | bytes 36868
  81.3 7.7 %copy-start.1 = (f32[3,128]{1,0:T(4,128)S(1)}, f32[3,128]{1,0:T(4,128)}, u32[]{:S(2)}) copy-start(f32[3,128]{1,0:T(4,128)} %get-tuple-element.12) | copy-start | bytes 4612

commit v2 on v1

--- a/solution.py
+++ b/solution.py
@@ -32,12 +32,13 @@
 
 def exchange_kernel(
     pair_map, indices, values, target, decoder,
-    recon, feat, error_out, acts_high_t, acts_low_t,
-    dec, dec_high, dec_low, ids_t, vals_t, acts_t, acts_high, acts_low,
-    map_send, map_rx, part_send, part_rx, part_own, plane_rx, layer_sum,
+    recon, feat, error_out, acts_high_out, acts_low_out,
+    acts_high_t, acts_low_t, dec, dec_high, dec_low, ids_t, vals_t, acts_t, acts_high, acts_low,
+    map_send, map_rx, part_send, part_rx, part_own, scale_send, scale_rx, plane_send, plane_rx, layer_sum,
+    line_wide,
     line_send, line_rx, err_send, err_rx, err_wide, err_layers, err_pick, err,
     back, picked, pick_rx, pick_line, feat_rx,
-    dec_sem, map_ssem, map_rsem, part_ssem, part_rsem, plane_ssem, plane_rsem,
+    dec_sem, out_sem, map_ssem, map_rsem, part_ssem, part_rsem, scale_ssem, scale_rsem, plane_ssem, plane_rsem,
     line_ssem, line_rsem, err_ssem, err_rsem, spread_ssem, spread_rsem,
     relay_ssem, relay_rsem, pick_ssem, pick_rsem, feat_ssem, feat_rsem,
 ):
@@ -48,12 +49,19 @@
     core = lax.rem(f, 2)
     q = p * 2 + y
 
-    def plane_peer(d):
-        q2 = lax.rem(q + d, PLANE)
-        return q2, (q2 // 2, lax.rem(q2, 2) * 16 + w)
-
-    def line_peer(d):
-        w2 = lax.rem(w + d, LINE)
+    def plane_peer(i):
+        a, b = i // 4, lax.rem(i, 4)
+        far = 2 + jnp.where(a == 1, 3, jnp.where(a == 2, 1, jnp.where(a == 3, 2, 0)))
+        x2 = lax.rem(lax.rem(p, 4) + far, 4)
+        low2 = lax.rem(p // 4 + jnp.where((b == 1) | (b == 2), 1, 0), 2)
+        y2 = lax.rem(y + jnp.where((b == 0) | (b == 2), 1, 0), 2)
+        p2 = low2 * 4 + x2
+        return p2 * 2 + y2, (p2, y2 * 16 + w)
+
+    def line_peer(i):
+        a, b = i // 2, lax.rem(i, 2)
+        far = 4 + jnp.where(lax.rem(a, 2) == 1, 8 - (a + 1) // 2, a // 2)
+        w2 = lax.rem(w // 2 + far, 8) * 2 + lax.rem(core + 1 - b, 2)
         return w2, (p, y * 16 + w2)
 
     partner = (p, f + 1 - 2 * core)
@@ -66,12 +74,10 @@
 
     barrier = pltpu.get_barrier_semaphore()
 
-    @pl.loop(1, 16)
+    @pl.loop(0, 15)
     def _(d):
         pl.semaphore_signal(barrier, inc=1, device_id=plane_peer(d)[1], device_id_type=MESH)
         pl.semaphore_signal(barrier, inc=1, device_id=line_peer(d)[1], device_id_type=MESH)
-
-    pl.semaphore_wait(barrier, 30)
 
     source = pair_map[0, 0]
     goal = pair_map[0, 1]
@@ -92,10 +98,6 @@
             src_ref=map_send, dst_ref=map_rx.at[p2], send_sem=map_ssem.at[p],
             recv_sem=map_rsem.at[p2], device_id=(p2, f), device_id_type=MESH)
 
-    @pl.loop(1, PAIRS)
-    def _(d):
-        map_copy(d).start()
-
     layer = jnp.minimum(source, LAYERS - 1)
     local = indices[layer] - f * WIDTH
     ids_t[...] = local.T
@@ -118,6 +120,13 @@
         high, low = split(total)
         acts_high_t[pl.ds(base, 64), :] = high
         acts_low_t[pl.ds(base, 64), :] = low
+
+    acts_copies = (
+        pltpu.make_async_copy(acts_high_t, acts_high_out, out_sem.at[0]),
+        pltpu.make_async_copy(acts_low_t, acts_low_out, out_sem.at[1]),
+    )
+    for copy in acts_copies:
+        copy.start()
 
     for block in range(WIDTH // 128):
         cols = slice(block * 128, block * 128 + 128)
@@ -146,99 +155,150 @@
             + jnp.dot(acts_high[...], dec_low[:, cols], preferred_element_type=F32)
         )
 
-    part_copy = pltpu.make_async_remote_copy(
-        src_ref=part_send, dst_ref=part_rx, send_sem=part_ssem, recv_sem=part_rsem,
-        device_id=partner, device_id_type=MESH)
+    def part_copy(n):
+        return pltpu.make_async_remote_copy(
+            src_ref=part_send.at[n], dst_ref=part_rx.at[n], send_sem=part_ssem.at[n],
+            recv_sem=part_rsem.at[n], device_id=partner, device_id_type=MESH)
+
+    part_send[0] = partial(pl.ds(pl.multiple_of((1 - core) * HALF, 256), 256))
+    pl.semaphore_wait(barrier, 30)
+    part_copy(0).start()
+
+    @pl.loop(1, PAIRS)
+    def _(d):
+        map_copy(d).start()
+
+    @pl.loop(1, HALF // 256)
+    def _(n):
+        part_send[n] = partial(pl.ds(pl.multiple_of((1 - core) * HALF + n * 256, 256), 256))
+        part_copy(n).start()
 
     @pl.loop(0, HALF // 256)
     def _(n):
-        cols = pl.ds(pl.multiple_of((1 - core) * HALF + n * 256, 256), 256)
-        part_send[:, pl.ds(pl.multiple_of(n * 256, 256), 256)] = partial(cols)
-
-    part_copy.start()
+        part_own[n] = partial(pl.ds(pl.multiple_of(core * HALF + n * 256, 256), 256))
 
     @pl.loop(0, HALF // 256)
     def _(n):
-        cols = pl.ds(pl.multiple_of(core * HALF + n * 256, 256), 256)
-        part_own[:, pl.ds(pl.multiple_of(n * 256, 256), 256)] = partial(cols)
-
-    part_copy.wait()
+        part_copy(n).wait_recv()
 
     def rows_of(q2):
         return pl.ds(pl.multiple_of(q2 * ROWS, ROWS), ROWS)
 
+    def scale_copy(d):
+        q2, peer = plane_peer(d)
+        return pltpu.make_async_remote_copy(
+            src_ref=scale_send.at[q2], dst_ref=scale_rx.at[q], send_sem=scale_ssem.at[q2],
+            recv_sem=scale_rsem.at[q], device_id=peer, device_id_type=MESH)
+
+    def scale_arrival(q2):
+        return pltpu.make_async_remote_copy(
+            src_ref=scale_send.at[q2], dst_ref=scale_rx.at[q2], send_sem=scale_ssem.at[q],
+            recv_sem=scale_rsem.at[q2], device_id=partner, device_id_type=MESH)
+
     def plane_copy(d):
         q2, peer = plane_peer(d)
         return pltpu.make_async_remote_copy(
-            src_ref=part_own.at[rows_of(q2)], dst_ref=plane_rx.at[q], send_sem=plane_ssem.at[q2],
+            src_ref=plane_send.at[q2], dst_ref=plane_rx.at[q], send_sem=plane_ssem.at[q2],
             recv_sem=plane_rsem.at[q], device_id=peer, device_id_type=MESH)
 
     def plane_arrival(q2):
         return pltpu.make_async_remote_copy(
-            src_ref=part_own.at[rows_of(q2)], dst_ref=plane_rx.at[q2], send_sem=plane_ssem.at[q],
+            src_ref=plane_send.at[q2], dst_ref=plane_rx.at[q2], send_sem=plane_ssem.at[q],
             recv_sem=plane_rsem.at[q2], device_id=partner, device_id_type=MESH)
 
-    @pl.loop(1, PLANE)
-    def _(d):
-        rows = rows_of(lax.rem(q + d, PLANE))
-        part_own[rows, :] = part_own[rows, :] + part_rx[rows, :]
+    def encode(q2):
+        rows = rows_of(q2)
+        parts = []
+        for n in range(HALF // 256):
+            x = part_own[n, rows, :] + part_rx[n, rows, :]
+            parts += [x[:, :128], x[:, 128:]]
+        peak = jnp.abs(parts[0])
+        for x in parts[1:]:
+            peak = jnp.maximum(peak, jnp.abs(x))
+        peak = jnp.maximum(jnp.max(peak, axis=0, keepdims=True), 1e-30)
+        inverse = 32000.0 / peak
+        codes = [jnp.round(x * inverse).astype(jnp.int16) for x in parts]
+        return codes, peak * (1.0 / 32000.0)
+
+    @pl.loop(0, 15)
+    def _(d):
+        q2 = plane_peer(d)[0]
+        codes, scale = encode(q2)
+        scale_send[q2] = scale
+        for m in range(8):
+            plane_send[q2, :, m * 128:m * 128 + 128] = codes[m]
+        scale_copy(d).start()
         plane_copy(d).start()
 
-    plane_rx[q] = part_own[rows_of(q), :] + part_rx[rows_of(q), :]
+    codes, scale = encode(q)
+    scale_rx[q] = scale
+    for m in range(8):
+        plane_rx[q, :, m * 128:m * 128 + 128] = codes[m]
 
     @pl.loop(1, PAIRS)
     def _(d):
         map_arrival(d).wait_recv()
 
-    @pl.loop(1, PLANE)
-    def _(d):
-        plane_arrival(lax.rem(q + d, PLANE)).wait_recv()
+    @pl.loop(0, 15)
+    def _(d):
+        plane_arrival(plane_peer(d)[0]).wait_recv()
+        scale_arrival(plane_peer(d)[0]).wait_recv()
 
     layer_sum[...] = jnp.zeros_like(layer_sum)
 
     @pl.loop(0, PAIRS)
     def _(p2):
-        both = plane_rx[2 * p2] + plane_rx[2 * p2 + 1]
+        scales = [jnp.concatenate([scale_rx[2 * p2 + k]] * 8, axis=1) for k in range(2)]
+        both = (
+            plane_rx[2 * p2].astype(F32) * scales[0] + plane_rx[2 * p2 + 1].astype(F32) * scales[1]
+        )
         goal2 = map_rx[p2, 4:5, 0:1]
         for l in range(LAYERS):
             layer_sum[l] += jnp.where(goal2 == l, both, 0.0)
 
     for l in range(LAYERS):
         for m in range(8):
-            line_send[pl.ds(l * 8 + m, 16, stride=24), :] = layer_sum[l, :, m * 128:m * 128 + 128]
-
-    def tile_of(w2):
-        return pl.ds(pl.multiple_of(w2 * 24, 8), 24)
+            line_wide[pl.ds(l * 8 + m, 16, stride=24), :] = layer_sum[l, :, m * 128:m * 128 + 128]
+
+    @pl.loop(0, LINE)
+    def _(w2):
+        x = line_wide[pl.ds(pl.multiple_of(w2 * 24, 8), 24), :]
+        peak = jnp.maximum(jnp.max(jnp.abs(x), axis=0, keepdims=True), 1e-30)
+        power = jnp.ceil(jnp.log2(peak * (1.0 / 32000.0)))
+        codes = jnp.round(x * jnp.exp2(-power))
+        line_send[w2] = jnp.concatenate(
+            [codes, jnp.broadcast_to(power, (8, 128))], axis=0).astype(jnp.int16)
 
     def line_copy(d):
         w2, peer = line_peer(d)
         return pltpu.make_async_remote_copy(
-            src_ref=line_send.at[tile_of(w2)], dst_ref=line_rx.at[w], send_sem=line_ssem.at[w2],
+            src_ref=line_send.at[w2], dst_ref=line_rx.at[w], send_sem=line_ssem.at[w2],
             recv_sem=line_rsem.at[w], device_id=peer, device_id_type=MESH)
 
     def line_arrival(w2):
         return pltpu.make_async_remote_copy(
-            src_ref=line_send.at[tile_of(w2)], dst_ref=line_rx.at[w2], send_sem=line_ssem.at[w],
+            src_ref=line_send.at[w2], dst_ref=line_rx.at[w2], send_sem=line_ssem.at[w],
             recv_sem=line_rsem.at[w2], device_id=partner, device_id_type=MESH)
 
-    @pl.loop(1, LINE)
+    @pl.loop(0, 15)
     def _(d):
         line_copy(d).start()
 
-    line_rx[w] = line_send[tile_of(w), :]
-
-    @pl.loop(1, LINE)
-    def _(d):
-        line_arrival(lax.rem(w + d, LINE)).wait_recv()
+    line_rx[w] = line_send[w]
+
+    @pl.loop(0, 15)
+    def _(d):
+        line_arrival(line_peer(d)[0]).wait_recv()
 
     for half in range(2):
-        total = line_rx[half]
-        for z2 in range(1, 8):
-            total = total + line_rx[2 * z2 + half]
+        total = jnp.zeros((24, 128), F32)
+        for z2 in range(8):
+            piece = line_rx[2 * z2 + half].astype(F32)
+            total = total + piece[0:24] * jnp.exp2(piece[24:25])
         for l in range(LAYERS):
             part = total[l * 8:l * 8 + 8]
             rows = slice(half * 8, half * 8 + 8)
-            recon[l, rows, :] = part.astype(BF16)
+            recon[l, rows, :] = part
             err_send[half, l * 8:l * 8 + 8, :] = (part - target[l, rows, :]).astype(BF16)
         err_send[half, 24:32, :] = jnp.zeros((8, 128), BF16)
 
@@ -253,15 +313,15 @@
             src_ref=err_send.at[0], dst_ref=err_rx.at[w2], send_sem=err_ssem.at[w],
             recv_sem=err_rsem.at[w2], device_id=partner, device_id_type=MESH)
 
-    @pl.loop(1, LINE)
+    @pl.loop(0, 15)
     def _(d):
         err_copy(d).start()
 
     err_rx[w] = err_send[core]
 
-    @pl.loop(1, LINE)
-    def _(d):
-        err_arrival(lax.rem(w + d, LINE)).wait_recv()
+    @pl.loop(0, 15)
+    def _(d):
+        err_arrival(line_peer(d)[0]).wait_recv()
 
     @pl.loop(0, LINE)
     def _(w2):
@@ -302,16 +362,16 @@
             src_ref=piece, dst_ref=piece, send_sem=relay_ssem.at[q2],
             recv_sem=relay_rsem.at[q2], device_id=partner, device_id_type=MESH)
 
-    @pl.loop(1, PLANE)
+    @pl.loop(0, 15)
     def _(d):
         spread_copy(d).start()
 
     err[core, rows_of(q), :] = err_pick[p]
     relay_copy(q).start()
 
-    @pl.loop(1, PLANE)
-    def _(d):
-        q2 = lax.rem(q + d, PLANE)
+    @pl.loop(0, 15)
+    def _(d):
+        q2 = plane_peer(d)[0]
         spread_arrival(q2).wait_recv()
         relay_copy(q2).start()
 
@@ -319,7 +379,8 @@
     def _(q2):
         relay_arrival(q2).wait_recv()
 
-    error_out[...] = err[...]
+    err_copy_out = pltpu.make_async_copy(err, error_out, out_sem.at[2])
+    err_copy_out.start()
 
     @pl.loop(0, WIDTH // 128)
     def _(n):
@@ -350,16 +411,16 @@
             src_ref=picked.at[rows_of(q2)], dst_ref=pick_rx.at[q2], send_sem=pick_ssem.at[q],
             recv_sem=pick_rsem.at[q2], device_id=partner, device_id_type=MESH)
 
-    @pl.loop(1, PLANE)
+    @pl.loop(0, 15)
     def _(d):
         pick_copy(d).start()
 
     pick_rx[q] = picked[rows_of(q), :]
     pick_line[...] = jnp.zeros_like(pick_line)
 
-    @pl.loop(1, PLANE)
-    def _(d):
-        pick_arrival(lax.rem(q + d, PLANE)).wait_recv()
+    @pl.loop(0, 15)
+    def _(d):
+        pick_arrival(plane_peer(d)[0]).wait_recv()
 
     sums = [jnp.zeros((ROWS, ACTIVE), F32) for _ in range(LAYERS)]
     for p2 in range(PAIRS):
@@ -381,27 +442,30 @@
             src_ref=pick_line.at[pl.ds(0, 8)], dst_ref=feat_rx.at[w2],
             send_sem=feat_ssem.at[w], recv_sem=feat_rsem.at[w2], device_id=partner, device_id_type=MESH)
 
-    @pl.loop(1, LINE)
+    @pl.loop(0, 15)
     def _(d):
         feat_copy(d).start()
 
     feat_rx[w] = pick_line[pl.ds(pl.multiple_of(w * 8, 8), 8), :]
 
-    @pl.loop(1, LINE)
-    def _(d):
-        feat_arrival(lax.rem(w + d, LINE)).wait_recv()
+    @pl.loop(0, 15)
+    def _(d):
+        feat_arrival(line_peer(d)[0]).wait_recv()
 
     total = feat_rx[0]
     for w2 in range(1, LINE):
         total = total + feat_rx[w2]
     feat[...] = total[0:LAYERS]
+    for copy in acts_copies + (err_copy_out,):
+        copy.wait()
 
     @pl.loop(1, PAIRS)
     def _(d):
         map_copy(d).wait_send()
 
-    @pl.loop(1, 16)
-    def _(d):
+    @pl.loop(0, 15)
+    def _(d):
+        scale_copy(d).wait_send()
         plane_copy(d).wait_send()
         line_copy(d).wait_send()
         err_copy(d).wait_send()
@@ -409,17 +473,25 @@
         pick_copy(d).wait_send()
         feat_copy(d).wait_send()
 
+    @pl.loop(0, HALF // 256)
+    def _(n):
+        part_copy(n).wait_send()
+
     @pl.loop(0, PLANE)
     def _(q2):
         relay_copy(q2).wait_send()
 
 
-def grad_kernel(acts_high_t, acts_low_t, err, out):
+def grad_kernel(acts_high_t, acts_low_t, err, recon, feat, out, recon_out, feat_out):
     e = err[0]
     out[...] = (
         jnp.dot(acts_high_t[...], e, preferred_element_type=F32)
         + jnp.dot(acts_low_t[...], e, preferred_element_type=F32)
     )
+    for k in range(16):
+        recon_out[:, k * 128:k * 128 + 128] = recon[:, k, :].astype(BF16)
+    for l in range(LAYERS):
+        feat_out[l] = feat[l:l + 1, :]
 
 
 def body(decoder, pair_map, indices, values, target):
@@ -428,15 +500,17 @@
     recon, feat, err, acts_high_t, acts_low_t = pl.pallas_call(
         exchange_kernel,
         out_shape=(
-            jax.ShapeDtypeStruct((LAYERS, 16, 128), BF16),
+            jax.ShapeDtypeStruct((LAYERS, 16, 128), F32),
             jax.ShapeDtypeStruct((LAYERS, ACTIVE), F32),
             jax.ShapeDtypeStruct((2, TOK, HALF), BF16),
             jax.ShapeDtypeStruct((WIDTH, TOK), BF16),
             jax.ShapeDtypeStruct((WIDTH, TOK), BF16),
         ),
         in_specs=[pl.BlockSpec(memory_space=pltpu.SMEM), vmem, vmem, vmem, pl.BlockSpec(memory_space=pl.ANY)],
-        out_specs=(vmem,) * 5,
+        out_specs=(vmem, vmem) + (pl.BlockSpec(memory_space=pl.ANY),) * 3,
         scratch_shapes=[
+            pltpu.VMEM((WIDTH, TOK), BF16),
+            pltpu.VMEM((WIDTH, TOK), BF16),
             pltpu.VMEM((WIDTH, MODEL), F32),
             pltpu.VMEM((WIDTH, MODEL), BF16),
             pltpu.VMEM((WIDTH, MODEL), BF16),
@@ -447,13 +521,17 @@
             pltpu.VMEM((TOK, WIDTH), BF16),
             pltpu.VMEM((8, 128), jnp.int32),
             pltpu.VMEM((PAIRS, 8, 128), jnp.int32),
-            pltpu.VMEM((TOK, HALF), F32),
-            pltpu.VMEM((TOK, HALF), F32),
-            pltpu.VMEM((TOK, HALF), F32),
-            pltpu.VMEM((PLANE, ROWS, HALF), F32),
+            pltpu.VMEM((HALF // 256, TOK, 256), F32),
+            pltpu.VMEM((HALF // 256, TOK, 256), F32),
+            pltpu.VMEM((HALF // 256, TOK, 256), F32),
+            pltpu.VMEM((PLANE, 1, 128), F32),
+            pltpu.VMEM((PLANE, 1, 128), F32),
+            pltpu.VMEM((PLANE, ROWS, HALF), jnp.int16),
+            pltpu.VMEM((PLANE, ROWS, HALF), jnp.int16),
             pltpu.VMEM((LAYERS, ROWS, HALF), F32),
             pltpu.VMEM((LINE * 24, 128), F32),
-            pltpu.VMEM((LINE, 24, 128), F32),
+            pltpu.VMEM((LINE, 32, 128), jnp.int16),
+            pltpu.VMEM((LINE, 32, 128), jnp.int16),
             pltpu.VMEM((2, 32, 128), BF16),
             pltpu.VMEM((LINE, 32, 128), BF16),
             pltpu.VMEM((LINE * 32, 128), F32),
@@ -465,9 +543,10 @@
             pltpu.VMEM((PLANE, ROWS, ACTIVE), F32),
             pltpu.VMEM((LINE * 8, 128), F32),
             pltpu.VMEM((LINE, 8, 128), F32),
-            dma((4,)),
+            dma((4,)), dma((3,)),
             dma((PAIRS,)), dma((PAIRS,)),
-            dma, dma,
+            dma((4,)), dma((4,)),
+            dma((PLANE,)), dma((PLANE,)),
             dma((PLANE,)), dma((PLANE,)),
             dma((LINE,)), dma((LINE,)),
             dma((LINE,)), dma((LINE,)),
@@ -480,22 +559,28 @@
             collective_id=0, has_side_effects=True, vmem_limit_bytes=56 * 2**20
         ),
     )(pair_map, indices, values, target.reshape(LAYERS, 16, 128), decoder)
-    dec_grad = pl.pallas_call(
+    dec_grad, recon, feat = pl.pallas_call(
         grad_kernel,
-        grid=(8,),
-        out_shape=jax.ShapeDtypeStruct((WIDTH, MODEL), F32),
+        grid=(2,),
+        out_shape=(
+            jax.ShapeDtypeStruct((WIDTH, MODEL), F32),
+            jax.ShapeDtypeStruct((LAYERS, MODEL), BF16),
+            jax.ShapeDtypeStruct((LAYERS, 1, ACTIVE), F32),
+        ),
         in_specs=[
             pl.BlockSpec((WIDTH, TOK), lambda n: (0, 0)),
             pl.BlockSpec((WIDTH, TOK), lambda n: (0, 0)),
-            pl.BlockSpec((1, TOK, 256), lambda n: (n // 4, 0, n % 4)),
+            pl.BlockSpec((1, TOK, HALF), lambda n: (n, 0, 0)),
+            pl.BlockSpec((LAYERS, 16, 128), lambda n: (0, 0, 0)),
+            pl.BlockSpec((LAYERS, ACTIVE), lambda n: (0, 0)),
         ],
-        out_specs=pl.BlockSpec((WIDTH, 256), lambda n: (0, n)),
-    )(acts_high_t, acts_low_t, err)
-    return (
-        recon.reshape(LAYERS, 1, MODEL),
-        dec_grad.reshape(1, WIDTH, MODEL),
-        feat.reshape(LAYERS, 1, ACTIVE),
-    )
+        out_specs=(
+            pl.BlockSpec((WIDTH, HALF), lambda n: (0, n)),
+            pl.BlockSpec((LAYERS, MODEL), lambda n: (0, 0)),
+            pl.BlockSpec((LAYERS, 1, ACTIVE), lambda n: (0, 0, 0)),
+        ),
+    )(acts_high_t, acts_low_t, err, recon, feat)
+    return recon.reshape(LAYERS, 1, MODEL), dec_grad.reshape(1, WIDTH, MODEL), feat
 
 
 def solution(mesh):

time: 89.8 us -> 72.8 us (0.81)
  Pallas kernels: 87.8 us -> 72 us
  local copies, waits for them, and re-layouts: 1.19 us -> 0 us
    pallas_call x1, Pallas kernels: 80.7 us -> 68 us  [body(): pl.pallas_call(exchange_kernel, out_shape=(jax.ShapeDtypeStruct((LAYERS,...]
    pallas_call x1, Pallas kernels: 7.06 us -> 3.99 us  [body(): pl.pallas_call(grad_kernel, grid=(2,), out_shape=(jax.ShapeDtypeStruct((W...]
where the time goes in v2:
time: 72.8 us; the launch traced here: 72.7 us
  Pallas kernels  72 us (99%)
    pallas_call x1, Pallas kernels, body(): pl.pallas_call(exchange_kernel, out_shape=(jax.ShapeDtypeStruct((LAYERS,...  68 us
    pallas_call x1, Pallas kernels, body(): pl.pallas_call(grad_kernel, grid=(2,), out_shape=(jax.ShapeDtypeStruct((W...  3.99 us

profile of v2, /device:TPU:1, one launch (start us, length us, event | category | flops | bytes accessed | tf_op | source)
XLA Modules:
  0.0 72.7 jit_solution(15176160709479299861)
XLA Ops:
  0.6 68.0 %shard_map.76 = (f32[3,16,128]{2,1,0:T(8,128)}, f32[3,128]{1,0:T(4,128)}, bf16[2,256,1024]{2,1,0:T(8,128)(2,1)}, bf16[512,256]{1,0:T(8,128)(2,1)}, bf16[512,256]{1,0:T(8,128)(2,1)}) custom-call(s32[1,2]{1,0:T(1,128)} %pair_map.1, s32[3,256,128]{2,1,0:T(8,128)} %indices.1, f32[3,256,128]{2,1,0:T(8,128)} %values.1, f32[3,16,128]{2,1,0:T(8,128)} %bitcast.3, ...), custom_call_target="tpu_custom_call" | custom-call | tf_op jit(solution)/shard_map/pallas_call | solution.py:500
  68.7 4.0 %shard_map.77 = (f32[512,2048]{1,0:T(8,128)}, bf16[3,2048]{1,0:T(4,128)(2,1)}, f32[3,1,128]{2,1,0:T(1,128)}) custom-call(bf16[512,256]{1,0:T(8,128)(2,1)} %get-tuple-element.11.acts_high_t, bf16[512,256]{1,0:T(8,128)(2,1)} %get-tuple-element.12.acts_low_t, bf16[2,256,1024]{2,1,0:T(8,128)(2,1)} %get-tuple-element.13.err, ...), custom_call_target="tpu_custom_call" | custom-call | tf_op jit(solution)/shard_map/pallas_call | solution.py:562

commit v3 on v2

--- a/solution.py
+++ b/solution.py
@@ -33,11 +33,11 @@
 def exchange_kernel(
     pair_map, indices, values, target, decoder,
     recon, feat, error_out, acts_high_out, acts_low_out,
-    acts_high_t, acts_low_t, dec, dec_high, dec_low, ids_t, vals_t, acts_t, acts_high, acts_low,
+    acts_high_t, acts_low_t, dec, dec_high, dec_low, ids_t, vals_t, acts,
     map_send, map_rx, part_send, part_rx, part_own, scale_send, scale_rx, plane_send, plane_rx, layer_sum,
     line_wide,
     line_send, line_rx, err_send, err_rx, err_wide, err_layers, err_pick, err,
-    back, picked, pick_rx, pick_line, feat_rx,
+    picked, pick_rx, pick_wide, pick_line, feat_rx,
     dec_sem, out_sem, map_ssem, map_rsem, part_ssem, part_rsem, scale_ssem, scale_rsem, plane_ssem, plane_rsem,
     line_ssem, line_rsem, err_ssem, err_rsem, spread_ssem, spread_rsem,
     relay_ssem, relay_rsem, pick_ssem, pick_rsem, feat_ssem, feat_rsem,
@@ -50,11 +50,11 @@
     q = p * 2 + y
 
     def plane_peer(i):
-        a, b = i // 4, lax.rem(i, 4)
+        same, a, b = i // 8, lax.rem(i, 8) // 2, lax.rem(i, 2)
         far = 2 + jnp.where(a == 1, 3, jnp.where(a == 2, 1, jnp.where(a == 3, 2, 0)))
         x2 = lax.rem(lax.rem(p, 4) + far, 4)
-        low2 = lax.rem(p // 4 + jnp.where((b == 1) | (b == 2), 1, 0), 2)
-        y2 = lax.rem(y + jnp.where((b == 0) | (b == 2), 1, 0), 2)
+        low2 = lax.rem(p // 4 + 1 - same, 2)
+        y2 = lax.rem(y + 1 - b, 2)
         p2 = low2 * 4 + x2
         return p2 * 2 + y2, (p2, y2 * 16 + w)
 
@@ -100,86 +100,9 @@
 
     layer = jnp.minimum(source, LAYERS - 1)
     local = indices[layer] - f * WIDTH
-    ids_t[...] = local.T
-    vals_t[...] = values[layer].T
-
-    @pl.loop(0, WIDTH // 64)
-    def _(block):
-        base = block * 64
-        features = lax.broadcasted_iota(jnp.int32, (64, TOK), 0) + base
-
-        def step(k, total):
-            for j in range(4):
-                ids = ids_t[pl.ds(k * 4 + j, 1), :]
-                vals = vals_t[pl.ds(k * 4 + j, 1), :]
-                total = jnp.where(ids == features, vals, total)
-            return total
-
-        total = lax.fori_loop(0, ACTIVE // 4, step, jnp.zeros((64, TOK), F32))
-        acts_t[pl.ds(base, 64), :] = total
-        high, low = split(total)
-        acts_high_t[pl.ds(base, 64), :] = high
-        acts_low_t[pl.ds(base, 64), :] = low
-
-    acts_copies = (
-        pltpu.make_async_copy(acts_high_t, acts_high_out, out_sem.at[0]),
-        pltpu.make_async_copy(acts_low_t, acts_low_out, out_sem.at[1]),
-    )
-    for copy in acts_copies:
-        copy.start()
-
-    for block in range(WIDTH // 128):
-        cols = slice(block * 128, block * 128 + 128)
-        high, low = split(acts_t[cols, :].T)
-        acts_high[:, cols] = high
-        acts_low[:, cols] = low
-
-    for block in range(4):
-        cols = pl.ds(block * 512, 512)
-        pltpu.make_async_copy(
-            decoder.at[0, :, cols], dec.at[:, cols], dec_sem.at[block]
-        ).wait()
-
-    @pl.loop(0, WIDTH // 16)
-    def _(block):
-        rows = pl.ds(block * 16, 16)
-        high, low = split(dec[rows, :])
-        dec_high[rows, :] = high
-        dec_low[rows, :] = low
-
-    def partial(cols):
-        high = dec_high[:, cols]
-        return (
-            jnp.dot(acts_high[...], high, preferred_element_type=F32)
-            + jnp.dot(acts_low[...], high, preferred_element_type=F32)
-            + jnp.dot(acts_high[...], dec_low[:, cols], preferred_element_type=F32)
-        )
-
-    def part_copy(n):
-        return pltpu.make_async_remote_copy(
-            src_ref=part_send.at[n], dst_ref=part_rx.at[n], send_sem=part_ssem.at[n],
-            recv_sem=part_rsem.at[n], device_id=partner, device_id_type=MESH)
-
-    part_send[0] = partial(pl.ds(pl.multiple_of((1 - core) * HALF, 256), 256))
-    pl.semaphore_wait(barrier, 30)
-    part_copy(0).start()
-
-    @pl.loop(1, PAIRS)
-    def _(d):
-        map_copy(d).start()
-
-    @pl.loop(1, HALF // 256)
-    def _(n):
-        part_send[n] = partial(pl.ds(pl.multiple_of((1 - core) * HALF + n * 256, 256), 256))
-        part_copy(n).start()
-
-    @pl.loop(0, HALF // 256)
-    def _(n):
-        part_own[n] = partial(pl.ds(pl.multiple_of(core * HALF + n * 256, 256), 256))
-
-    @pl.loop(0, HALF // 256)
-    def _(n):
-        part_copy(n).wait_recv()
+    for k in range(2):
+        ids_t[k] = local[k * 128:k * 128 + 128].T
+        vals_t[k] = values[layer, k * 128:k * 128 + 128, :].T
 
     def rows_of(q2):
         return pl.ds(pl.multiple_of(q2 * ROWS, ROWS), ROWS)
@@ -220,15 +143,97 @@
         codes = [jnp.round(x * inverse).astype(jnp.int16) for x in parts]
         return codes, peak * (1.0 / 32000.0)
 
-    @pl.loop(0, 15)
-    def _(d):
-        q2 = plane_peer(d)[0]
-        codes, scale = encode(q2)
-        scale_send[q2] = scale
-        for m in range(8):
-            plane_send[q2, :, m * 128:m * 128 + 128] = codes[m]
-        scale_copy(d).start()
-        plane_copy(d).start()
+    def partial(cols):
+        both = jnp.dot(acts[...], dec_high[:, cols], preferred_element_type=F32)
+        rest = jnp.dot(acts[0:TOK // 2, :], dec_low[:, cols], preferred_element_type=F32)
+        return both[0:TOK // 2] + both[TOK // 2:] + rest
+
+    def tokens_of(same):
+        low2 = p // 4 + (1 - 2 * (p // 4)) * (1 - same)
+        return low2, pl.ds(pl.multiple_of(low2 * 128, 128), 128)
+
+    def part_copy(same, n):
+        tokens = tokens_of(same)[1]
+        return pltpu.make_async_remote_copy(
+            src_ref=part_send.at[n, tokens], dst_ref=part_rx.at[n, tokens],
+            send_sem=part_ssem.at[same * 4 + n], recv_sem=part_rsem.at[same * 4 + n],
+            device_id=partner, device_id_type=MESH)
+
+    for same in range(2):
+        low2, tokens = tokens_of(same)
+
+        @pl.loop(0, WIDTH // 128)
+        def _(block):
+            base = pl.multiple_of(block * 128, 128)
+            features = lax.broadcasted_iota(jnp.int32, (128, 128), 0) + base
+
+            def step(k, total):
+                for j in range(4):
+                    ids = ids_t[low2, pl.ds(k * 4 + j, 1), :]
+                    vals = vals_t[low2, pl.ds(k * 4 + j, 1), :]
+                    total = jnp.where(ids == features, vals, total)
+                return total
+
+            total = lax.fori_loop(0, ACTIVE // 4, step, jnp.zeros((128, 128), F32))
+            high, low = split(total)
+            acts_high_t[pl.ds(base, 128), tokens] = high
+            acts_low_t[pl.ds(base, 128), tokens] = low
+            high, low = split(total.T)
+            cols = pl.ds(pl.multiple_of(base, 128), 128)
+            acts[0:TOK // 2, cols] = high
+            acts[TOK // 2:, cols] = low
+
+        if same == 0:
+            for block in range(4):
+                cols = pl.ds(block * 512, 512)
+                pltpu.make_async_copy(
+                    decoder.at[0, :, cols], dec.at[:, cols], dec_sem.at[block]
+                ).wait()
+
+            @pl.loop(0, WIDTH // 16)
+            def _(block):
+                rows = pl.ds(block * 16, 16)
+                high, low = split(dec[rows, :])
+                dec_high[rows, :] = high
+                dec_low[rows, :] = low
+
+            part_send[0, tokens, :] = partial(pl.ds(pl.multiple_of((1 - core) * HALF, 256), 256))
+            pl.semaphore_wait(barrier, 30)
+            part_copy(0, 0).start()
+
+            @pl.loop(1, PAIRS)
+            def _(d):
+                map_copy(d).start()
+
+        @pl.loop(1 - same, HALF // 256)
+        def _(n):
+            part_send[n, tokens, :] = partial(pl.ds(pl.multiple_of((1 - core) * HALF + n * 256, 256), 256))
+            part_copy(same, n).start()
+
+        @pl.loop(0, HALF // 256)
+        def _(n):
+            part_own[n, tokens, :] = partial(pl.ds(pl.multiple_of(core * HALF + n * 256, 256), 256))
+
+        @pl.loop(0, HALF // 256)
+        def _(n):
+            part_copy(same, n).wait_recv()
+
+        @pl.loop(8 * same, 8 + 7 * same)
+        def _(d):
+            q2 = plane_peer(d)[0]
+            codes, scale = encode(q2)
+            scale_send[q2] = scale
+            for m in range(8):
+                plane_send[q2, :, m * 128:m * 128 + 128] = codes[m]
+            scale_copy(d).start()
+            plane_copy(d).start()
+
+    acts_copies = (
+        pltpu.make_async_copy(acts_high_t, acts_high_out, out_sem.at[0]),
+        pltpu.make_async_copy(acts_low_t, acts_low_out, out_sem.at[1]),
+    )
+    for copy in acts_copies:
+        copy.start()
 
     codes, scale = encode(q)
     scale_rx[q] = scale
@@ -239,35 +244,42 @@
     def _(d):
         map_arrival(d).wait_recv()
 
-    @pl.loop(0, 15)
-    def _(d):
-        plane_arrival(plane_peer(d)[0]).wait_recv()
-        scale_arrival(plane_peer(d)[0]).wait_recv()
-
     layer_sum[...] = jnp.zeros_like(layer_sum)
 
-    @pl.loop(0, PAIRS)
-    def _(p2):
-        scales = [jnp.concatenate([scale_rx[2 * p2 + k]] * 8, axis=1) for k in range(2)]
-        both = (
-            plane_rx[2 * p2].astype(F32) * scales[0] + plane_rx[2 * p2 + 1].astype(F32) * scales[1]
-        )
-        goal2 = map_rx[p2, 4:5, 0:1]
+    def add_pair(q2, q3):
+        scales = [jnp.concatenate([scale_rx[k]] * 8, axis=1) for k in (q2, q3)]
+        both = plane_rx[q2].astype(F32) * scales[0] + plane_rx[q3].astype(F32) * scales[1]
+        goal2 = map_rx[q2 // 2, 4:5, 0:1]
         for l in range(LAYERS):
             layer_sum[l] += jnp.where(goal2 == l, both, 0.0)
 
-    for l in range(LAYERS):
-        for m in range(8):
-            line_wide[pl.ds(l * 8 + m, 16, stride=24), :] = layer_sum[l, :, m * 128:m * 128 + 128]
-
-    @pl.loop(0, LINE)
-    def _(w2):
-        x = line_wide[pl.ds(pl.multiple_of(w2 * 24, 8), 24), :]
-        peak = jnp.maximum(jnp.max(jnp.abs(x), axis=0, keepdims=True), 1e-30)
-        power = jnp.ceil(jnp.log2(peak * (1.0 / 32000.0)))
-        codes = jnp.round(x * jnp.exp2(-power))
-        line_send[w2] = jnp.concatenate(
-            [codes, jnp.broadcast_to(power, (8, 128))], axis=0).astype(jnp.int16)
+    def wait_plane(q2):
+        plane_arrival(q2).wait_recv()
+        scale_arrival(q2).wait_recv()
+
+    @pl.loop(0, 7)
+    def _(j):
+        q2, q3 = plane_peer(2 * j)[0], plane_peer(2 * j + 1)[0]
+        wait_plane(q2)
+        wait_plane(q3)
+        add_pair(q2, q3)
+
+    q2 = plane_peer(14)[0]
+    wait_plane(q2)
+    add_pair(q2, q)
+
+    tiles = [(l, m, layer_sum[l, :, m * 128:m * 128 + 128]) for l in range(LAYERS) for m in range(8)]
+    peak = jnp.full((ROWS, 128), 1e-30, F32)
+    for _, _, x in tiles:
+        peak = jnp.maximum(peak, jnp.abs(x))
+    power = jnp.ceil(jnp.log2(peak * (1.0 / 32000.0)))
+    inverse = jnp.exp2(-power)
+    for l, m, x in tiles:
+        line_wide[pl.ds(l * 8 + m, 16, stride=32), :] = jnp.round(x * inverse)
+    for m in range(8):
+        line_wide[pl.ds(24 + m, 16, stride=32), :] = power
+    for w2 in range(LINE):
+        line_send[w2] = line_wide[w2 * 32:w2 * 32 + 32, :].astype(jnp.int16)
 
     def line_copy(d):
         w2, peer = line_peer(d)
@@ -300,7 +312,6 @@
             rows = slice(half * 8, half * 8 + 8)
             recon[l, rows, :] = part
             err_send[half, l * 8:l * 8 + 8, :] = (part - target[l, rows, :]).astype(BF16)
-        err_send[half, 24:32, :] = jnp.zeros((8, 128), BF16)
 
     def err_copy(d):
         w2, peer = line_peer(d)
@@ -325,98 +336,102 @@
 
     @pl.loop(0, LINE)
     def _(w2):
-        err_wide[pl.ds(pl.multiple_of(w2 * 32, 32), 32), :] = err_rx[w2].astype(F32)
+        err_wide[pl.ds(pl.multiple_of(w2 * 24, 8), 24), :] = err_rx[w2].astype(F32)
 
     for l in range(LAYERS):
         for m in range(8):
-            err_layers[l, :, m * 128:m * 128 + 128] = err_wide[pl.ds(l * 8 + m, 16, stride=32), :]
-
-    @pl.loop(0, PAIRS)
-    def _(p2):
+            err_layers[l, :, m * 128:m * 128 + 128] = err_wide[pl.ds(l * 8 + m, 16, stride=24), :]
+
+    def spread_copy(d):
+        q2, peer = plane_peer(d)
+        return pltpu.make_async_remote_copy(
+            src_ref=err_pick.at[q2 // 2], dst_ref=err.at[core, rows_of(q)], send_sem=spread_ssem.at[q2],
+            recv_sem=spread_rsem.at[q], device_id=peer, device_id_type=MESH)
+
+    def spread_arrival(q2):
+        return pltpu.make_async_remote_copy(
+            src_ref=err_pick.at[0], dst_ref=err.at[core, rows_of(q2)], send_sem=spread_ssem.at[q],
+            recv_sem=spread_rsem.at[q2], device_id=partner, device_id_type=MESH)
+
+    def relay_copy(q2):
+        piece = err.at[core, rows_of(q2)]
+        return pltpu.make_async_remote_copy(
+            src_ref=piece, dst_ref=piece, send_sem=relay_ssem.at[q2],
+            recv_sem=relay_rsem.at[q2], device_id=partner, device_id_type=MESH)
+
+    def relay_arrival(q2):
+        piece = err.at[1 - core, rows_of(q2)]
+        return pltpu.make_async_remote_copy(
+            src_ref=piece, dst_ref=piece, send_sem=relay_ssem.at[q2],
+            recv_sem=relay_rsem.at[q2], device_id=partner, device_id_type=MESH)
+
+    def choose(p2):
         goal2 = map_rx[p2, 4:5, 0:1]
         chosen = jnp.zeros((ROWS, HALF), F32)
         for l in range(LAYERS):
             chosen = jnp.where(goal2 == l, err_layers[l], chosen)
         err_pick[p2] = chosen.astype(BF16)
 
-    def spread_copy(d):
-        q2, peer = plane_peer(d)
-        return pltpu.make_async_remote_copy(
-            src_ref=err_pick.at[q2 // 2], dst_ref=err.at[core, rows_of(q)], send_sem=spread_ssem.at[q2],
-            recv_sem=spread_rsem.at[q], device_id=peer, device_id_type=MESH)
-
-    def spread_arrival(q2):
-        return pltpu.make_async_remote_copy(
-            src_ref=err_pick.at[0], dst_ref=err.at[core, rows_of(q2)], send_sem=spread_ssem.at[q],
-            recv_sem=spread_rsem.at[q2], device_id=partner, device_id_type=MESH)
-
-    def relay_copy(q2):
-        piece = err.at[core, rows_of(q2)]
-        return pltpu.make_async_remote_copy(
-            src_ref=piece, dst_ref=piece, send_sem=relay_ssem.at[q2],
-            recv_sem=relay_rsem.at[q2], device_id=partner, device_id_type=MESH)
-
-    def relay_arrival(q2):
-        piece = err.at[1 - core, rows_of(q2)]
-        return pltpu.make_async_remote_copy(
-            src_ref=piece, dst_ref=piece, send_sem=relay_ssem.at[q2],
-            recv_sem=relay_rsem.at[q2], device_id=partner, device_id_type=MESH)
-
-    @pl.loop(0, 15)
-    def _(d):
-        spread_copy(d).start()
-
+    @pl.loop(0, 7)
+    def _(j):
+        choose(plane_peer(2 * j)[0] // 2)
+        spread_copy(2 * j).start()
+        spread_copy(2 * j + 1).start()
+
+    choose(p)
+    spread_copy(14).start()
     err[core, rows_of(q), :] = err_pick[p]
     relay_copy(q).start()
 
-    @pl.loop(0, 15)
-    def _(d):
-        q2 = plane_peer(d)[0]
-        spread_arrival(q2).wait_recv()
-        relay_copy(q2).start()
-
-    @pl.loop(0, PLANE)
-    def _(q2):
-        relay_arrival(q2).wait_recv()
+    def pick_copy(d):
+        q2, peer = plane_peer(d)
+        return pltpu.make_async_remote_copy(
+            src_ref=picked.at[rows_of(q2)], dst_ref=pick_rx.at[q], send_sem=pick_ssem.at[q2],
+            recv_sem=pick_rsem.at[q], device_id=peer, device_id_type=MESH)
+
+    def pick_arrival(q2):
+        return pltpu.make_async_remote_copy(
+            src_ref=picked.at[rows_of(q2)], dst_ref=pick_rx.at[q2], send_sem=pick_ssem.at[q],
+            recv_sem=pick_rsem.at[q2], device_id=partner, device_id_type=MESH)
+
+    for same in range(2):
+        last = 8 + 7 * same
+        low2, tokens = tokens_of(same)
+
+        @pl.loop(8 * same, last)
+        def _(d):
+            q2 = plane_peer(d)[0]
+            spread_arrival(q2).wait_recv()
+            relay_copy(q2).start()
+
+        @pl.loop(0, 8)
+        def _(k):
+            relay_arrival(low2 * 8 + k).wait_recv()
+
+        local = indices[layer, tokens, :] - f * WIDTH
+        lane = jnp.bitwise_and(local, 127)
+        block_of = jnp.right_shift(local, 7)
+        found = jnp.zeros((TOK // 2, ACTIVE), F32)
+        for n in range(WIDTH // 256):
+            rows = slice(n * 256, n * 256 + 256)
+            back = jnp.zeros((TOK // 2, 256), F32)
+            for half in range(2):
+                cols = slice(half * HALF, half * HALF + HALF)
+                e = err[half, tokens, :]
+                back = back + nt(e, dec_high[rows, cols]) + nt(e, dec_low[rows, cols])
+            for k in range(2):
+                here = jnp.take_along_axis(back[:, k * 128:k * 128 + 128], lane, axis=1)
+                found = jnp.where(block_of == 2 * n + k, here, found)
+        picked[tokens, :] = found
+
+        @pl.loop(8 * same, last)
+        def _(d):
+            pick_copy(d).start()
 
     err_copy_out = pltpu.make_async_copy(err, error_out, out_sem.at[2])
     err_copy_out.start()
-
-    @pl.loop(0, WIDTH // 128)
-    def _(n):
-        rows = pl.ds(pl.multiple_of(n * 128, 128), 128)
-        total = jnp.zeros((TOK, 128), F32)
-        for half in range(2):
-            cols = slice(half * HALF, half * HALF + HALF)
-            total = total + nt(err[half], dec_high[rows, cols]) + nt(err[half], dec_low[rows, cols])
-        back[n] = total
-
-    local = indices[layer] - f * WIDTH
-    lane = jnp.bitwise_and(local, 127)
-    block_of = jnp.right_shift(local, 7)
-    found = jnp.zeros((TOK, ACTIVE), F32)
-    for n in range(WIDTH // 128):
-        here = jnp.take_along_axis(back[n], lane, axis=1)
-        found = jnp.where(block_of == n, here, found)
-    picked[...] = found
-
-    def pick_copy(d):
-        q2, peer = plane_peer(d)
-        return pltpu.make_async_remote_copy(
-            src_ref=picked.at[rows_of(q2)], dst_ref=pick_rx.at[q], send_sem=pick_ssem.at[q2],
-            recv_sem=pick_rsem.at[q], device_id=peer, device_id_type=MESH)
-
-    def pick_arrival(q2):
-        return pltpu.make_async_remote_copy(
-            src_ref=picked.at[rows_of(q2)], dst_ref=pick_rx.at[q2], send_sem=pick_ssem.at[q],
-            recv_sem=pick_rsem.at[q2], device_id=partner, device_id_type=MESH)
-
-    @pl.loop(0, 15)
-    def _(d):
-        pick_copy(d).start()
-
     pick_rx[q] = picked[rows_of(q), :]
-    pick_line[...] = jnp.zeros_like(pick_line)
+    pick_wide[...] = jnp.zeros_like(pick_wide)
 
     @pl.loop(0, 15)
     def _(d):
@@ -429,24 +444,27 @@
         for l in range(LAYERS):
             sums[l] = sums[l] + jnp.where(source2 == l, both, 0.0)
     for l in range(LAYERS):
-        pick_line[pl.ds(l, 16, stride=8), :] = sums[l]
+        pick_wide[pl.ds(l, 16, stride=8), :] = sums[l]
+
+    for w2 in range(LINE):
+        pick_line[w2] = pick_wide[w2 * 8:w2 * 8 + 4, :]
 
     def feat_copy(d):
         w2, peer = line_peer(d)
         return pltpu.make_async_remote_copy(
-            src_ref=pick_line.at[pl.ds(pl.multiple_of(w2 * 8, 8), 8)], dst_ref=feat_rx.at[w],
+            src_ref=pick_line.at[w2], dst_ref=feat_rx.at[w],
             send_sem=feat_ssem.at[w2], recv_sem=feat_rsem.at[w], device_id=peer, device_id_type=MESH)
 
     def feat_arrival(w2):
         return pltpu.make_async_remote_copy(
-            src_ref=pick_line.at[pl.ds(0, 8)], dst_ref=feat_rx.at[w2],
+            src_ref=pick_line.at[w2], dst_ref=feat_rx.at[w2],
             send_sem=feat_ssem.at[w], recv_sem=feat_rsem.at[w2], device_id=partner, device_id_type=MESH)
 
     @pl.loop(0, 15)
     def _(d):
         feat_copy(d).start()
 
-    feat_rx[w] = pick_line[pl.ds(pl.multiple_of(w * 8, 8), 8), :]
+    feat_rx[w] = pick_line[w]
 
     @pl.loop(0, 15)
     def _(d):
@@ -475,7 +493,8 @@
 
     @pl.loop(0, HALF // 256)
     def _(n):
-        part_copy(n).wait_send()
+        part_copy(0, n).wait_send()
+        part_copy(1, n).wait_send()
 
     @pl.loop(0, PLANE)
     def _(q2):
@@ -514,10 +533,8 @@
             pltpu.VMEM((WIDTH, MODEL), F32),
             pltpu.VMEM((WIDTH, MODEL), BF16),
             pltpu.VMEM((WIDTH, MODEL), BF16),
-            pltpu.VMEM((ACTIVE, TOK), jnp.int32),
-            pltpu.VMEM((ACTIVE, TOK), F32),
-            pltpu.VMEM((WIDTH, TOK), F32),
-            pltpu.VMEM((TOK, WIDTH), BF16),
+            pltpu.VMEM((2, ACTIVE, TOK // 2), jnp.int32),
+            pltpu.VMEM((2, ACTIVE, TOK // 2), F32),
             pltpu.VMEM((TOK, WIDTH), BF16),
             pltpu.VMEM((8, 128), jnp.int32),
             pltpu.VMEM((PAIRS, 8, 128), jnp.int32),
@@ -529,23 +546,23 @@
             pltpu.VMEM((PLANE, ROWS, HALF), jnp.int16),
             pltpu.VMEM((PLANE, ROWS, HALF), jnp.int16),
             pltpu.VMEM((LAYERS, ROWS, HALF), F32),
-            pltpu.VMEM((LINE * 24, 128), F32),
+            pltpu.VMEM((LINE * 32, 128), F32),
             pltpu.VMEM((LINE, 32, 128), jnp.int16),
             pltpu.VMEM((LINE, 32, 128), jnp.int16),
-            pltpu.VMEM((2, 32, 128), BF16),
-            pltpu.VMEM((LINE, 32, 128), BF16),
-            pltpu.VMEM((LINE * 32, 128), F32),
+            pltpu.VMEM((2, 24, 128), BF16),
+            pltpu.VMEM((LINE, 24, 128), BF16),
+            pltpu.VMEM((LINE * 24, 128), F32),
             pltpu.VMEM((LAYERS, ROWS, HALF), F32),
             pltpu.VMEM((PAIRS, ROWS, HALF), BF16),
             pltpu.VMEM((2, TOK, HALF), BF16),
-            pltpu.VMEM((WIDTH // 128, TOK, 128), F32),
             pltpu.VMEM((TOK, ACTIVE), F32),
             pltpu.VMEM((PLANE, ROWS, ACTIVE), F32),
             pltpu.VMEM((LINE * 8, 128), F32),
-            pltpu.VMEM((LINE, 8, 128), F32),
+            pltpu.VMEM((LINE, 4, 128), F32),
+            pltpu.VMEM((LINE, 4, 128), F32),
             dma((4,)), dma((3,)),
             dma((PAIRS,)), dma((PAIRS,)),
-            dma((4,)), dma((4,)),
+            dma((8,)), dma((8,)),
             dma((PLANE,)), dma((PLANE,)),
             dma((PLANE,)), dma((PLANE,)),
             dma((LINE,)), dma((LINE,)),

time: 72.8 us -> 70.7 us (0.971)
  Pallas kernels: 72 us -> 70 us
    pallas_call x1, Pallas kernels: 68 us -> 66 us  [body(): pl.pallas_call(exchange_kernel, out_shape=(jax.ShapeDtypeStruct((LAYERS,...]
where the time goes in v3:
time: 70.7 us; the launch traced here: 70.6 us
  Pallas kernels  70 us (99%)
    pallas_call x1, Pallas kernels, body(): pl.pallas_call(exchange_kernel, out_shape=(jax.ShapeDtypeStruct((LAYERS,...  66 us
    pallas_call x1, Pallas kernels, body(): pl.pallas_call(grad_kernel, grid=(2,), out_shape=(jax.ShapeDtypeStruct((W...  3.99 us

profile of v3, /device:TPU:1, one launch (start us, length us, event | category | flops | bytes accessed | tf_op | source)
XLA Modules:
  0.0 70.6 jit_solution(17562873823938481501)
XLA Ops:
  0.6 66.0 %shard_map.76 = (f32[3,16,128]{2,1,0:T(8,128)}, f32[3,128]{1,0:T(4,128)}, bf16[2,256,1024]{2,1,0:T(8,128)(2,1)}, bf16[512,256]{1,0:T(8,128)(2,1)}, bf16[512,256]{1,0:T(8,128)(2,1)}) custom-call(s32[1,2]{1,0:T(1,128)} %pair_map.1, s32[3,256,128]{2,1,0:T(8,128)} %indices.1, f32[3,256,128]{2,1,0:T(8,128)} %values.1, f32[3,16,128]{2,1,0:T(8,128)} %bitcast.3, ...), custom_call_target="tpu_custom_call" | custom-call | tf_op jit(solution)/shard_map/pallas_call | solution.py:519
  66.6 4.0 %shard_map.77 = (f32[512,2048]{1,0:T(8,128)}, bf16[3,2048]{1,0:T(4,128)(2,1)}, f32[3,1,128]{2,1,0:T(1,128)}) custom-call(bf16[512,256]{1,0:T(8,128)(2,1)} %get-tuple-element.11.acts_high_t, bf16[512,256]{1,0:T(8,128)(2,1)} %get-tuple-element.12.acts_low_t, bf16[2,256,1024]{2,1,0:T(8,128)(2,1)} %get-tuple-element.13.err, ...), custom_call_target="tpu_custom_call" | custom-call | tf_op jit(solution)/shard_map/pallas_call | solution.py:579

commit v4 on v3

--- a/solution.py
+++ b/solution.py
@@ -32,13 +32,13 @@
 
 def exchange_kernel(
     pair_map, indices, values, target, decoder,
-    recon, feat, error_out, acts_high_out, acts_low_out,
+    recon, feat, grad,
     acts_high_t, acts_low_t, dec, dec_high, dec_low, ids_t, vals_t, acts,
     map_send, map_rx, part_send, part_rx, part_own, scale_send, scale_rx, plane_send, plane_rx, layer_sum,
     line_wide,
     line_send, line_rx, err_send, err_rx, err_wide, err_layers, err_pick, err,
-    picked, pick_rx, pick_wide, pick_line, feat_rx,
-    dec_sem, out_sem, map_ssem, map_rsem, part_ssem, part_rsem, scale_ssem, scale_rsem, plane_ssem, plane_rsem,
+    back, picked, pick_rx, pick_wide, pick_line, feat_rx,
+    dec_sem, map_ssem, map_rsem, part_ssem, part_rsem, scale_ssem, scale_rsem, plane_ssem, plane_rsem,
     line_ssem, line_rsem, err_ssem, err_rsem, spread_ssem, spread_rsem,
     relay_ssem, relay_rsem, pick_ssem, pick_rsem, feat_ssem, feat_rsem,
 ):
@@ -132,9 +132,9 @@
     def encode(q2):
         rows = rows_of(q2)
         parts = []
-        for n in range(HALF // 256):
-            x = part_own[n, rows, :] + part_rx[n, rows, :]
-            parts += [x[:, :128], x[:, 128:]]
+        for m in range(8):
+            cols = slice(m * 128, m * 128 + 128)
+            parts.append(part_own[rows, cols] + part_rx[rows, cols])
         peak = jnp.abs(parts[0])
         for x in parts[1:]:
             peak = jnp.maximum(peak, jnp.abs(x))
@@ -152,11 +152,11 @@
         low2 = p // 4 + (1 - 2 * (p // 4)) * (1 - same)
         return low2, pl.ds(pl.multiple_of(low2 * 128, 128), 128)
 
-    def part_copy(same, n):
+    def part_copy(same):
         tokens = tokens_of(same)[1]
         return pltpu.make_async_remote_copy(
-            src_ref=part_send.at[n, tokens], dst_ref=part_rx.at[n, tokens],
-            send_sem=part_ssem.at[same * 4 + n], recv_sem=part_rsem.at[same * 4 + n],
+            src_ref=part_send.at[tokens], dst_ref=part_rx.at[tokens],
+            send_sem=part_ssem.at[same], recv_sem=part_rsem.at[same],
             device_id=partner, device_id_type=MESH)
 
     for same in range(2):
@@ -197,26 +197,20 @@
                 dec_high[rows, :] = high
                 dec_low[rows, :] = low
 
-            part_send[0, tokens, :] = partial(pl.ds(pl.multiple_of((1 - core) * HALF, 256), 256))
+        part_send[tokens, :] = partial(pl.ds(pl.multiple_of((1 - core) * HALF, HALF), HALF))
+
+        if same == 0:
             pl.semaphore_wait(barrier, 30)
-            part_copy(0, 0).start()
-
+
+        part_copy(same).start()
+
+        if same == 0:
             @pl.loop(1, PAIRS)
             def _(d):
                 map_copy(d).start()
 
-        @pl.loop(1 - same, HALF // 256)
-        def _(n):
-            part_send[n, tokens, :] = partial(pl.ds(pl.multiple_of((1 - core) * HALF + n * 256, 256), 256))
-            part_copy(same, n).start()
-
-        @pl.loop(0, HALF // 256)
-        def _(n):
-            part_own[n, tokens, :] = partial(pl.ds(pl.multiple_of(core * HALF + n * 256, 256), 256))
-
-        @pl.loop(0, HALF // 256)
-        def _(n):
-            part_copy(same, n).wait_recv()
+        part_own[tokens, :] = partial(pl.ds(pl.multiple_of(core * HALF, HALF), HALF))
+        part_copy(same).wait_recv()
 
         @pl.loop(8 * same, 8 + 7 * same)
         def _(d):
@@ -227,13 +221,6 @@
                 plane_send[q2, :, m * 128:m * 128 + 128] = codes[m]
             scale_copy(d).start()
             plane_copy(d).start()
-
-    acts_copies = (
-        pltpu.make_async_copy(acts_high_t, acts_high_out, out_sem.at[0]),
-        pltpu.make_async_copy(acts_low_t, acts_low_out, out_sem.at[1]),
-    )
-    for copy in acts_copies:
-        copy.start()
 
     codes, scale = encode(q)
     scale_rx[q] = scale
@@ -394,42 +381,43 @@
             src_ref=picked.at[rows_of(q2)], dst_ref=pick_rx.at[q2], send_sem=pick_ssem.at[q],
             recv_sem=pick_rsem.at[q2], device_id=partner, device_id_type=MESH)
 
-    for same in range(2):
-        last = 8 + 7 * same
-        low2, tokens = tokens_of(same)
-
-        @pl.loop(8 * same, last)
-        def _(d):
-            q2 = plane_peer(d)[0]
-            spread_arrival(q2).wait_recv()
-            relay_copy(q2).start()
-
-        @pl.loop(0, 8)
-        def _(k):
-            relay_arrival(low2 * 8 + k).wait_recv()
-
-        local = indices[layer, tokens, :] - f * WIDTH
-        lane = jnp.bitwise_and(local, 127)
-        block_of = jnp.right_shift(local, 7)
-        found = jnp.zeros((TOK // 2, ACTIVE), F32)
-        for n in range(WIDTH // 256):
-            rows = slice(n * 256, n * 256 + 256)
-            back = jnp.zeros((TOK // 2, 256), F32)
-            for half in range(2):
-                cols = slice(half * HALF, half * HALF + HALF)
-                e = err[half, tokens, :]
-                back = back + nt(e, dec_high[rows, cols]) + nt(e, dec_low[rows, cols])
-            for k in range(2):
-                here = jnp.take_along_axis(back[:, k * 128:k * 128 + 128], lane, axis=1)
-                found = jnp.where(block_of == 2 * n + k, here, found)
-        picked[tokens, :] = found
-
-        @pl.loop(8 * same, last)
-        def _(d):
-            pick_copy(d).start()
-
-    err_copy_out = pltpu.make_async_copy(err, error_out, out_sem.at[2])
-    err_copy_out.start()
+    def back_of(half):
+        cols = pl.ds(pl.multiple_of(half * HALF, HALF), HALF)
+        e = err[half]
+        return nt(e, dec_high[:, cols]) + nt(e, dec_low[:, cols])
+
+    @pl.loop(0, 15)
+    def _(d):
+        q2 = plane_peer(d)[0]
+        spread_arrival(q2).wait_recv()
+        relay_copy(q2).start()
+
+    back[...] = back_of(core)
+
+    @pl.loop(0, PLANE)
+    def _(q2):
+        relay_arrival(q2).wait_recv()
+
+    back[...] += back_of(1 - core)
+    local = indices[layer] - f * WIDTH
+    lane = jnp.bitwise_and(local, 127)
+    block_of = jnp.right_shift(local, 7)
+    found = jnp.zeros((TOK, ACTIVE), F32)
+    for n in range(WIDTH // 128):
+        here = jnp.take_along_axis(back[:, n * 128:n * 128 + 128], lane, axis=1)
+        found = jnp.where(block_of == n, here, found)
+    picked[...] = found
+
+    @pl.loop(0, 15)
+    def _(d):
+        pick_copy(d).start()
+
+    for half in range(2):
+        cols = slice(half * HALF, half * HALF + HALF)
+        e = err[half]
+        grad[:, cols] = jnp.dot(acts_high_t[...], e, preferred_element_type=F32) + jnp.dot(
+            acts_low_t[...], e, preferred_element_type=F32)
+
     pick_rx[q] = picked[rows_of(q), :]
     pick_wide[...] = jnp.zeros_like(pick_wide)
 
@@ -474,8 +462,6 @@
     for w2 in range(1, LINE):
         total = total + feat_rx[w2]
     feat[...] = total[0:LAYERS]
-    for copy in acts_copies + (err_copy_out,):
-        copy.wait()
 
     @pl.loop(1, PAIRS)
     def _(d):
@@ -491,42 +477,42 @@
         pick_copy(d).wait_send()
         feat_copy(d).wait_send()
 
-    @pl.loop(0, HALF // 256)
-    def _(n):
-        part_copy(0, n).wait_send()
-        part_copy(1, n).wait_send()
+    for same in range(2):
+        part_copy(same).wait_send()
 
     @pl.loop(0, PLANE)
     def _(q2):
         relay_copy(q2).wait_send()
 
 
-def grad_kernel(acts_high_t, acts_low_t, err, recon, feat, out, recon_out, feat_out):
-    e = err[0]
-    out[...] = (
-        jnp.dot(acts_high_t[...], e, preferred_element_type=F32)
-        + jnp.dot(acts_low_t[...], e, preferred_element_type=F32)
-    )
+def output_kernel(grad, recon, feat, out, recon_out, feat_out, sem):
+    copies = [
+        pltpu.make_async_copy(
+            grad.at[pl.ds(k * 128, 128)], out.at[pl.ds(k * 128, 128)], sem.at[k])
+        for k in range(WIDTH // 128)
+    ]
+    for copy in copies:
+        copy.start()
     for k in range(16):
         recon_out[:, k * 128:k * 128 + 128] = recon[:, k, :].astype(BF16)
     for l in range(LAYERS):
         feat_out[l] = feat[l:l + 1, :]
+    for copy in copies:
+        copy.wait()
 
 
 def body(decoder, pair_map, indices, values, target):
     vmem = pl.BlockSpec(memory_space=pltpu.VMEM)
     dma = pltpu.SemaphoreType.DMA
-    recon, feat, err, acts_high_t, acts_low_t = pl.pallas_call(
+    recon, feat, grad = pl.pallas_call(
         exchange_kernel,
         out_shape=(
-            jax.ShapeDtypeStruct((LAYERS, 16, 128), F32),
-            jax.ShapeDtypeStruct((LAYERS, ACTIVE), F32),
-            jax.ShapeDtypeStruct((2, TOK, HALF), BF16),
-            jax.ShapeDtypeStruct((WIDTH, TOK), BF16),
-            jax.ShapeDtypeStruct((WIDTH, TOK), BF16),
+            pltpu.VMEM((LAYERS, 16, 128), F32),
+            pltpu.VMEM((LAYERS, ACTIVE), F32),
+            pltpu.VMEM((WIDTH, MODEL), F32),
         ),
         in_specs=[pl.BlockSpec(memory_space=pltpu.SMEM), vmem, vmem, vmem, pl.BlockSpec(memory_space=pl.ANY)],
-        out_specs=(vmem, vmem) + (pl.BlockSpec(memory_space=pl.ANY),) * 3,
+        out_specs=(vmem, vmem, vmem),
         scratch_shapes=[
             pltpu.VMEM((WIDTH, TOK), BF16),
             pltpu.VMEM((WIDTH, TOK), BF16),
@@ -538,9 +524,9 @@
             pltpu.VMEM((TOK, WIDTH), BF16),
             pltpu.VMEM((8, 128), jnp.int32),
             pltpu.VMEM((PAIRS, 8, 128), jnp.int32),
-            pltpu.VMEM((HALF // 256, TOK, 256), F32),
-            pltpu.VMEM((HALF // 256, TOK, 256), F32),
-            pltpu.VMEM((HALF // 256, TOK, 256), F32),
+            pltpu.VMEM((TOK, HALF), F32),
+            pltpu.VMEM((TOK, HALF), F32),
+            pltpu.VMEM((TOK, HALF), F32),
             pltpu.VMEM((PLANE, 1, 128), F32),
             pltpu.VMEM((PLANE, 1, 128), F32),
             pltpu.VMEM((PLANE, ROWS, HALF), jnp.int16),
@@ -555,14 +541,15 @@
             pltpu.VMEM((LAYERS, ROWS, HALF), F32),
             pltpu.VMEM((PAIRS, ROWS, HALF), BF16),
             pltpu.VMEM((2, TOK, HALF), BF16),
+            pltpu.VMEM((TOK, WIDTH), F32),
             pltpu.VMEM((TOK, ACTIVE), F32),
             pltpu.VMEM((PLANE, ROWS, ACTIVE), F32),
             pltpu.VMEM((LINE * 8, 128), F32),
             pltpu.VMEM((LINE, 4, 128), F32),
             pltpu.VMEM((LINE, 4, 128), F32),
-            dma((4,)), dma((3,)),
+            dma((4,)),
             dma((PAIRS,)), dma((PAIRS,)),
-            dma((8,)), dma((8,)),
+            dma((2,)), dma((2,)),
             dma((PLANE,)), dma((PLANE,)),
             dma((PLANE,)), dma((PLANE,)),
             dma((LINE,)), dma((LINE,)),
@@ -573,30 +560,21 @@
             dma((LINE,)), dma((LINE,)),
         ],
         compiler_params=pltpu.CompilerParams(
-            collective_id=0, has_side_effects=True, vmem_limit_bytes=56 * 2**20
+            collective_id=0, has_side_effects=True, vmem_limit_bytes=59 * 2**20
         ),
     )(pair_map, indices, values, target.reshape(LAYERS, 16, 128), decoder)
     dec_grad, recon, feat = pl.pallas_call(
-        grad_kernel,
-        grid=(2,),
+        output_kernel,
         out_shape=(
             jax.ShapeDtypeStruct((WIDTH, MODEL), F32),
             jax.ShapeDtypeStruct((LAYERS, MODEL), BF16),
             jax.ShapeDtypeStruct((LAYERS, 1, ACTIVE), F32),
         ),
-        in_specs=[
-            pl.BlockSpec((WIDTH, TOK), lambda n: (0, 0)),
-            pl.BlockSpec((WIDTH, TOK), lambda n: (0, 0)),
-            pl.BlockSpec((1, TOK, HALF), lambda n: (n, 0, 0)),
-            pl.BlockSpec((LAYERS, 16, 128), lambda n: (0, 0, 0)),
-            pl.BlockSpec((LAYERS, ACTIVE), lambda n: (0, 0)),
-        ],
-        out_specs=(
-            pl.BlockSpec((WIDTH, HALF), lambda n: (0, n)),
-            pl.BlockSpec((LAYERS, MODEL), lambda n: (0, 0)),
-            pl.BlockSpec((LAYERS, 1, ACTIVE), lambda n: (0, 0, 0)),
-        ),
-    )(acts_high_t, acts_low_t, err, recon, feat)
+        in_specs=[vmem, vmem, vmem],
+        out_specs=(pl.BlockSpec(memory_space=pl.ANY), vmem, vmem),
+        scratch_shapes=[dma((WIDTH // 128,))],
+        compiler_params=pltpu.CompilerParams(vmem_limit_bytes=59 * 2**20),
+    )(*(pltpu.with_memory_space_constraint(x, pltpu.VMEM) for x in (grad, recon, feat)))
     return recon.reshape(LAYERS, 1, MODEL), dec_grad.reshape(1, WIDTH, MODEL), feat
 
 

time: 70.7 us -> 66.1 us (0.935)
  Pallas kernels: 70 us -> 65.3 us
    pallas_call x2, Pallas kernels: 70 us -> 65.3 us  [the longest x1 62.7 us: body(): pl.pallas_call(exchange_kernel, out_shape=(pltpu.VMEM((LAYERS, 16, 128),...]
where the time goes in v4:
time: 66.1 us; the launch traced here: 66 us
  Pallas kernels  65.3 us (99%)
    pallas_call x1, Pallas kernels, body(): pl.pallas_call(exchange_kernel, out_shape=(pltpu.VMEM((LAYERS, 16, 128),...  62.7 us
    pallas_call x1, Pallas kernels, body(): pl.pallas_call(output_kernel, out_shape=(jax.ShapeDtypeStruct((WIDTH, MOD...  2.65 us

profile of v4, /device:TPU:1, one launch (start us, length us, event | category | flops | bytes accessed | tf_op | source)
XLA Modules:
  0.0 66.0 jit_solution(11510429465259165154)
XLA Ops:
  0.6 62.7 %shard_map.76 = (f32[3,16,128]{2,1,0:T(8,128)S(1)}, f32[3,128]{1,0:T(4,128)S(1)}, f32[512,2048]{1,0:T(8,128)S(1)}) custom-call(s32[1,2]{1,0:T(1,128)} %pair_map.1, s32[3,256,128]{2,1,0:T(8,128)} %indices.1, f32[3,256,128]{2,1,0:T(8,128)} %values.1, f32[3,16,128]{2,1,0:T(8,128)} %bitcast.3, f32[1,512,2048]{2,1,0:T(8,128)} %decoder.1), custom_call_target="tpu_custom_call" | custom-call | tf_op jit(solution)/shard_map/pallas_call | solution.py:507
  63.3 2.6 %shard_map.77 = (f32[512,2048]{1,0:T(8,128)}, bf16[3,2048]{1,0:T(4,128)(2,1)}, f32[3,1,128]{2,1,0:T(1,128)}) custom-call(f32[512,2048]{1,0:T(8,128)S(1)} %get-tuple-element.9.grad, f32[3,16,128]{2,1,0:T(8,128)S(1)} %get-tuple-element.10.recon, f32[3,128]{1,0:T(4,128)S(1)} %get-tuple-element.11.feat), custom_call_target="tpu_custom_call" | custom-call | tf_op jit(solution)/shard_map/pallas_call | solution.py:566

commit v5 on v4

--- a/solution.py
+++ b/solution.py
@@ -168,13 +168,13 @@
             features = lax.broadcasted_iota(jnp.int32, (128, 128), 0) + base
 
             def step(k, total):
-                for j in range(4):
-                    ids = ids_t[low2, pl.ds(k * 4 + j, 1), :]
-                    vals = vals_t[low2, pl.ds(k * 4 + j, 1), :]
+                for j in range(16):
+                    ids = ids_t[low2, pl.ds(k * 16 + j, 1), :]
+                    vals = vals_t[low2, pl.ds(k * 16 + j, 1), :]
                     total = jnp.where(ids == features, vals, total)
                 return total
 
-            total = lax.fori_loop(0, ACTIVE // 4, step, jnp.zeros((128, 128), F32))
+            total = lax.fori_loop(0, ACTIVE // 16, step, jnp.zeros((128, 128), F32))
             high, low = split(total)
             acts_high_t[pl.ds(base, 128), tokens] = high
             acts_low_t[pl.ds(base, 128), tokens] = low

time: 66.1 us -> 65 us (0.983)
  Pallas kernels: 65.3 us -> 64.3 us
    pallas_call x1, Pallas kernels: 62.7 us -> 61.6 us  [body(): pl.pallas_call(exchange_kernel, out_shape=(pltpu.VMEM((LAYERS, 16, 128),...]
where the time goes in v5:
time: 65 us; the launch traced here: 64.9 us
  Pallas kernels  64.3 us (99%)
    pallas_call x1, Pallas kernels, body(): pl.pallas_call(exchange_kernel, out_shape=(pltpu.VMEM((LAYERS, 16, 128),...  61.6 us
    pallas_call x1, Pallas kernels, body(): pl.pallas_call(output_kernel, out_shape=(jax.ShapeDtypeStruct((WIDTH, MOD...  2.65 us

profile of v5, /device:TPU:1, one launch (start us, length us, event | category | flops | bytes accessed | tf_op | source)
XLA Modules:
  0.0 64.9 jit_solution(11149783231047429532)
XLA Ops:
  0.6 61.6 %shard_map.76 = (f32[3,16,128]{2,1,0:T(8,128)S(1)}, f32[3,128]{1,0:T(4,128)S(1)}, f32[512,2048]{1,0:T(8,128)S(1)}) custom-call(s32[1,2]{1,0:T(1,128)} %pair_map.1, s32[3,256,128]{2,1,0:T(8,128)} %indices.1, f32[3,256,128]{2,1,0:T(8,128)} %values.1, f32[3,16,128]{2,1,0:T(8,128)} %bitcast.3, f32[1,512,2048]{2,1,0:T(8,128)} %decoder.1), custom_call_target="tpu_custom_call" | custom-call | tf_op jit(solution)/shard_map/pallas_call | solution.py:507
  62.2 2.6 %shard_map.77 = (f32[512,2048]{1,0:T(8,128)}, bf16[3,2048]{1,0:T(4,128)(2,1)}, f32[3,1,128]{2,1,0:T(1,128)}) custom-call(f32[512,2048]{1,0:T(8,128)S(1)} %get-tuple-element.9.grad, f32[3,16,128]{2,1,0:T(8,128)S(1)} %get-tuple-element.10.recon, f32[3,128]{1,0:T(4,128)S(1)} %get-tuple-element.11.feat), custom_call_target="tpu_custom_call" | custom-call | tf_op jit(solution)/shard_map/pallas_call | solution.py:566
